TPU v7x, 128 devices: a whole 4x4x4 slice. The times are simulated.
128 devices in a mesh: row: 8 (over y, core), col: 16 (over x, z).
Axes of the slice: x: 4, y: 4, z: 4, core: 2. Of those that a mesh axis runs over, the one named last changes fastest.
Arguments:
- object_field: float32 [2, 1024, 2048], P(None, 'row', 'col'), may hold values from -4 to 4
- probe_modes: float32 [8, 2, 128, 128], replicated, may hold values from -1.5 to 1.5
- coefficients: float32 [8, 16, 32, 8], P('row', 'col'), may hold values from -4 to 4
- offsets: int32 [8, 16, 32, 2], P('row', 'col'), may hold values from 0 to 128
- counts: int32 [8, 16], P('row', 'col'), may hold values from 16 to 32
- measured: int32 [8, 16, 32, 128, 128], P('row', 'col'), may hold values from 0 to 4095
Outputs:
- object_out: float32 [2, 1024, 2048], P(None, 'row', 'col')
- modes_out: float32 [8, 2, 128, 128], replicated
- coefficients_out: float32 [8, 16, 32, 8], P('row', 'col')
All inputs are finite; a program needn't handle non-finite values.
Results may differ from a plain program's by a relative error of at most 0.0003.
Values sent between devices are 32-bit elements; how exact they have to be, the bound alone decides.
No kernel may reach another device: no remote copies, remote signals or barrier semaphores. Data moves between devices by JAX's collectives and lax.ppermute only.
A program may use at most 128 MiB of HBM per device.

v0:
```python
import math

import jax
import jax.numpy as jnp
import numpy as np
from jax import lax
from jax.experimental import pallas as pl
from jax.experimental.pallas import tpu as pltpu
from jax.sharding import PartitionSpec as P

PS = 128
MODES = 8
TILE = 128
PMAX = 32
ITERS = 2
EXT = TILE + PS
F32 = jnp.float32
BF16 = jnp.bfloat16
PAIRS = 4
LEAD = 33
ROWS = PS // 2
MARGIN = PS // 2


def split(x):
    hi = x.astype(BF16)
    lo = (x - hi.astype(F32)).astype(BF16)
    return hi, lo


def triple(x, axis):
    hi, lo = split(x)
    return jnp.concatenate([hi, lo, hi], axis=axis)


def dft_constants():
    ramp = np.arange(PS)
    angles = (ramp[:, None] * ramp[None, :] % PS) * (2.0 * math.pi / PS)
    cos = np.cos(angles) / math.sqrt(PS)
    sin = -np.sin(angles) / math.sqrt(PS)
    parts = []
    for table in (np.block([[cos, sin], [-sin, cos]]), np.block([[cos, -sin], [sin, cos]])):
        table = table.astype(np.float32)
        hi = table.astype(jnp.bfloat16)
        parts += [hi, (table - hi.astype(np.float32)).astype(jnp.bfloat16)]
    return np.stack(parts)


def dot(a, b):
    return jnp.dot(a, b, preferred_element_type=F32)


def live_only(coef, counts):
    slot = lax.broadcasted_iota(jnp.int32, coef.shape, 1)
    return jnp.where(slot < counts[0, 0], coef[...], 0.0)


def probe_kernel(base, counts, modes, coef, *refs):
    probe_r, probe_i = refs[-2:]
    left = triple(live_only(coef, counts).T, 1)

    def rows(y, _):
        m = modes[y]
        h = m.astype(BF16).astype(F32)
        right = jnp.concatenate([h, h, m - h], axis=0).astype(BF16)
        out = dot(left, right)
        start = (base[0] + y) * LEAD
        probe_r[pl.ds(start, PMAX), :] = out[:, :PS]
        probe_i[pl.ds(start, PMAX), :] = out[:, PS:]
        return 0

    lax.fori_loop(0, modes.shape[0], rows, 0, unroll=8)


def wave_kernel(half, counts, offs, *refs):
    (
        photons, probe_r, probe_i, coef, tables,
        up, mid, down, out_r, out_i, out_p, near, far,
        acc_rl, acc_rh, acc_il, acc_ih, acc_pl, acc_ph,
        patches, wave, field, cross_r, cross_i, power, sems, ext,
    ) = refs[-27:]
    pieces = refs[:-27]
    step = pl.program_id(0)
    lane = lax.broadcasted_iota(jnp.int32, (PS, PS), 1)
    if len(pieces) == 1:
        ext = pieces[0]
    sums = ((acc_rl, acc_rh), (acc_il, acc_ih), (acc_pl, acc_ph))

    @pl.when(step == 0)
    def _():
        if len(pieces) == 3:
            row = 0
            for piece in pieces:
                ext[:, :, row : row + piece.shape[2]] = piece[...]
                row += piece.shape[2]
        for low, high in sums:
            low[...] = jnp.zeros_like(low)
            high[...] = jnp.zeros_like(high)

    def own_lanes(left):
        return (lane < left + MARGIN) & (lane >= left - MARGIN)

    def regroup(x):
        top = jnp.concatenate([x[:PS, :PS], x[PS:, :PS]], axis=1)
        low = jnp.concatenate([x[:PS, PS:], x[PS:, PS:]], axis=1)
        return jnp.concatenate([top, low], axis=0)

    def take(j, q):
        p = 2 * PAIRS * step + 2 * j + q
        return (
            probe_r[pl.ds(p, PS, stride=LEAD), :],
            probe_i[pl.ds(p, PS, stride=LEAD), :],
            patches[2 * j + q, 0],
            patches[2 * j + q, 1],
        )

    def cut(j, q):
        p = 2 * PAIRS * step + 2 * j + q
        top = offs[0, p]
        left = offs[1, p]
        turn = (PS + MARGIN - left) & (PS - 1)
        inside = own_lanes(left)
        total = None
        for c in range(2):
            patch = jnp.where(
                inside, ext[c, 0, pl.ds(top, PS), :], ext[c, 1, pl.ds(top, PS), :]
            )
            patch = pltpu.roll(patch, turn, 1)
            patches[2 * j + q, c] = patch
            total = patch * patch if total is None else total + patch * patch
        power[pl.ds(p, PS, stride=LEAD), :] = total

    def start(j):
        for q in range(2):
            cut(j, q)
            pr, pi, obj_r, obj_i = take(j, q)
            rows = slice(q * PS, (q + 1) * PS)
            wave[j, rows, :PS] = pr * obj_r - pi * obj_i
            wave[j, rows, PS:] = pr * obj_i + pi * obj_r

    def correct(j, there):
        count = jnp.concatenate([photons[2 * j], photons[2 * j + 1]], axis=1).astype(F32)
        far_r = there[:PS]
        far_i = there[PS:]
        size = jnp.maximum(far_r * far_r + far_i * far_i, 0.25)
        scale = count * lax.rsqrt(jnp.maximum(count * size, 0.0625)) * 0.03125
        return jnp.concatenate([far_r * scale, far_i * scale], axis=0)

    def finish(j):
        for q in range(2):
            p = 2 * PAIRS * step + 2 * j + q
            top = offs[0, p]
            left = offs[1, p]
            turn = (left + MARGIN) & (PS - 1)
            inside = own_lanes(left)
            rows = slice(q * PS, (q + 1) * PS)
            diff_r = field[j, rows, :PS]
            diff_i = field[j, rows, PS:]
            pr, pi, obj_r, obj_i = take(j, q)
            cross_r[pl.ds(p, PS, stride=LEAD), :] = obj_r * diff_r + obj_i * diff_i
            cross_i[pl.ds(p, PS, stride=LEAD), :] = obj_r * diff_i - obj_i * diff_r
            pieces = (
                pr * diff_r + pi * diff_i,
                pr * diff_i - pi * diff_r,
                pr * pr + pi * pi,
            )
            for (low, high), piece in zip(sums, pieces):
                turned = pltpu.roll(piece, turn, 1)
                near = jnp.where(inside, turned, 0.0)
                low[pl.ds(top, PS), :] += near
                high[pl.ds(top, PS), :] += turned - near

    def table(i, axis):
        hi = tables[2 * i]
        return jnp.concatenate([hi, hi, tables[2 * i + 1]], axis=axis)

    pairs = range(PAIRS)
    for j in pairs:
        start(j)
    x = [dot(triple(wave[j], 1), table(0, 0)) for j in pairs]
    x = [dot(table(1, 1), triple(regroup(x[j]), 0)) for j in pairs]
    x = [correct(j, x[j]) for j in pairs]
    x = [dot(table(0, 1), triple(x[j], 0)) for j in pairs]
    for j in pairs:
        field[j] = dot(triple(regroup(x[j]), 1), table(1, 0)) - wave[j]
    for j in pairs:
        finish(j)

    @pl.when(step == PMAX // (2 * PAIRS) - 1)
    def _():
        width = up.shape[1]
        moves = [(cross_r, out_r), (cross_i, out_i), (power, out_p)]
        for i, piece in enumerate((acc_rl, acc_il, acc_pl, acc_rh, acc_ih, acc_ph)):
            moves.append((piece.at[:width], down.at[i]))
            moves.append((piece.at[EXT - width:], up.at[i]))
            if width < PS:
                moves.append((piece.at[width : EXT - width], mid.at[i]))
        copies = [
            pltpu.make_async_copy(source, target, sems.at[i])
            for i, (source, target) in enumerate(moves)
        ]
        for copy in copies:
            copy.start()

        def stacked(x):
            hi, lo = split(x)
            zero = jnp.zeros_like(hi)
            return jnp.concatenate(
                [jnp.concatenate([hi, hi], axis=1), jnp.concatenate([lo, zero], axis=1)], axis=0
            )

        used = live_only(coef, counts)
        left = stacked(used)
        left_square = stacked(used * used)
        for target, base in ((near, half[0] * ROWS), (far, (1 - half[0]) * ROWS)):

            def rows(y, _):
                begin = (base + y) * LEAD
                pair = jnp.concatenate(
                    [cross_r[pl.ds(begin, PMAX), :], cross_i[pl.ds(begin, PMAX), :]], axis=1
                )
                h, l = split(pair)
                out = dot(left, jnp.concatenate([h, l], axis=0))
                target[y, :, : 2 * PS] = out[:MODES] + out[MODES:]
                h, l = split(power[pl.ds(begin, PMAX), :])
                out = dot(left_square, jnp.concatenate([h, l], axis=0))
                target[y, :, 2 * PS:] = out[:MODES] + out[MODES:]
                return 0

            lax.fori_loop(0, ROWS, rows, 0, unroll=8)
        for copy in copies:
            copy.wait()


CHUNK = 64


def coef_kernel(cross_r, cross_i, powers, modes, coef, out, num, den):
    step = pl.program_id(0)

    @pl.when(step == 0)
    def _():
        num[...] = jnp.zeros_like(num)
        den[...] = jnp.zeros_like(den)

    dims = (((1,), (1,)), ((), ()))

    def wide_dot(a, b):
        return lax.dot_general(a, b, dims, preferred_element_type=F32)

    top = jnp.zeros((PMAX, MODES), F32)
    low = jnp.zeros((PMAX, MODES), F32)
    for y in range(CHUNK):
        rows = slice(y * LEAD, y * LEAD + PMAX)
        cross = jnp.concatenate([cross_r[rows, :], cross_i[rows, :]], axis=1)
        m = modes[y]
        power = m[:, :PS] * m[:, :PS] + m[:, PS:] * m[:, PS:]
        h, l = split(m)
        top += wide_dot(triple(cross, 1), jnp.concatenate([h, h, l], axis=1))
        h, l = split(power)
        low += wide_dot(triple(powers[rows, :], 1), jnp.concatenate([h, h, l], axis=1))
    num[...] += top
    den[...] += low

    @pl.when(step == PS // CHUNK - 1)
    def _():
        out[...] = coef[...] + (num[...] / (den[...] + 1.0)).T


def update_kernel(got, mine, new, copies):
    total = jnp.sum(got[...], axis=0)
    power = total[:, 2 * PS:] + 1.0
    row = mine[...] + total[:, : 2 * PS] / jnp.concatenate([power, power], axis=1)
    new[...] = row
    copies[...] = jnp.broadcast_to(row[None], copies.shape)


def beside_kernel(block, right, left, both, first, last):
    lane = lax.broadcasted_iota(jnp.int32, (PS, PS), 1)
    for c in range(2):
        beside = jnp.where(lane < MARGIN, right[c], left[c])
        for i, plane in ((0, block[c]), (1, beside)):
            both[c, i] = plane
            first[c, i] = plane[:MARGIN]
            last[c, i] = plane[MARGIN:]


def rows_kernel(up, down, from_above, from_below, full, to_right, to_left):
    lane = lax.broadcasted_iota(jnp.int32, (PS, PS), 1)
    for c in range(3):
        for rows, own, other in ((slice(0, PS), down, from_above), (slice(PS, EXT), up, from_below)):
            centre = own[c] + other[c]
            beside = own[3 + c] + other[3 + c]
            full[c, rows] = centre
            full[3 + c, rows] = beside
            to_right[c, rows] = jnp.where(lane < MARGIN, beside, centre)
            to_left[c, rows] = jnp.where(lane < MARGIN, centre, beside)


SMEM = pl.BlockSpec(memory_space=pltpu.SMEM)
VMEM = pl.BlockSpec(memory_space=pltpu.VMEM)


def mix_probes(base, counts, modes, coef, *before):
    grid = jax.ShapeDtypeStruct((PS * LEAD, PS), F32)
    return pl.pallas_call(
        probe_kernel,
        out_shape=(grid, grid),
        in_specs=[SMEM, SMEM, VMEM, VMEM, *[VMEM] * len(before)],
        out_specs=(VMEM, VMEM),
        input_output_aliases={4: 0, 5: 1} if before else {},
        compiler_params=pltpu.CompilerParams(vmem_limit_bytes=2 << 20),
        name="probes",
    )(base, counts, modes, coef, *before)


def sum_rows(up, down, from_above, from_below):
    side = jax.ShapeDtypeStruct((3, EXT, PS), F32)
    return pl.pallas_call(
        rows_kernel,
        out_shape=(jax.ShapeDtypeStruct((6, EXT, PS), F32), side, side),
        in_specs=[VMEM] * 4,
        out_specs=(VMEM,) * 3,
        compiler_params=pltpu.CompilerParams(vmem_limit_bytes=2 << 20),
        name="rows",
    )(up, down, from_above, from_below)


def waves(half, counts, offs, pieces, photons, probe_r, probe_i, coef, tables, width):
    edge = pltpu.HBM((6, width, PS), F32)
    inner = pltpu.HBM((6, max(EXT - 2 * width, 8), PS), F32)
    grid = pltpu.HBM((PS * LEAD, PS), F32)
    rows = jax.ShapeDtypeStruct((ROWS, MODES, 3 * PS), F32)
    square = pltpu.VMEM((PAIRS, 2 * PS, 2 * PS), F32)
    return pl.pallas_call(
        wave_kernel,
        grid=(PMAX // (2 * PAIRS),),
        out_shape=(edge, inner, edge, *[grid] * 3, rows, rows),
        in_specs=[
            SMEM,
            SMEM,
            SMEM,
            *[VMEM] * len(pieces),
            pl.BlockSpec((2 * PAIRS, PS, PS), lambda i: (i, 0, 0)),
            VMEM,
            VMEM,
            VMEM,
            VMEM,
        ],
        out_specs=(*[pl.BlockSpec(memory_space=pltpu.HBM)] * 6, VMEM, VMEM),
        scratch_shapes=[
            *[pltpu.VMEM((EXT, PS), F32)] * 6,
            pltpu.VMEM((2 * PAIRS, 2, PS, PS), F32),
            square,
            square,
            *[pltpu.VMEM((PS * LEAD, PS), F32)] * 3,
            pltpu.SemaphoreType.DMA((21,)),
            pltpu.VMEM((2, 2, EXT, PS), F32),
        ],
        compiler_params=pltpu.CompilerParams(
            dimension_semantics=("arbitrary",), vmem_limit_bytes=24 << 20
        ),
        name="waves",
    )(half, counts, offs, *pieces, photons, probe_r, probe_i, coef, tables)


def new_coefficients(cross_r, cross_i, powers, modes, coef):
    rows = pl.BlockSpec((CHUNK * LEAD, PS), lambda i: (i, 0))
    whole = pl.BlockSpec((MODES, PMAX), lambda i: (0, 0))
    return pl.pallas_call(
        coef_kernel,
        grid=(PS // CHUNK,),
        out_shape=jax.ShapeDtypeStruct((MODES, PMAX), F32),
        in_specs=[
            rows,
            rows,
            rows,
            pl.BlockSpec((CHUNK, MODES, 2 * PS), lambda i: (i, 0, 0)),
            whole,
        ],
        out_specs=whole,
        scratch_shapes=[pltpu.VMEM((PMAX, MODES), F32)] * 2,
        compiler_params=pltpu.CompilerParams(
            dimension_semantics=("arbitrary",), vmem_limit_bytes=56 << 20
        ),
        name="coefs",
    )(cross_r, cross_i, powers, modes, coef)


def update_row(got, mine):
    return pl.pallas_call(
        update_kernel,
        out_shape=(
            jax.ShapeDtypeStruct((MODES, 2 * PS), F32),
            jax.ShapeDtypeStruct((ROWS, MODES, 2 * PS), F32),
        ),
        in_specs=[VMEM, VMEM],
        out_specs=(VMEM, VMEM),
        compiler_params=pltpu.CompilerParams(vmem_limit_bytes=2 << 20),
        name="update",
    )(got, mine)


def shifted(x, move):
    rows, cols = lax.axis_size("row"), lax.axis_size("col")
    pairs = []
    for a in range(rows):
        for b in range(cols):
            c, d = a + move[0], b + move[1]
            if 0 <= c < rows and 0 <= d < cols:
                pairs.append((c * cols + d, a * cols + b))
    return lax.ppermute(x, ("row", "col"), pairs)


def by_side(low, high):
    lane = lax.broadcasted_iota(jnp.int32, low.shape, low.ndim - 1)
    return jnp.where(lane < MARGIN, low, high)


def extend(block, modes):
    right, left, modes = lax.optimization_barrier(
        (shifted(block, (0, 1)), shifted(block, (0, -1)), modes)
    )
    strip = jax.ShapeDtypeStruct((2, 2, MARGIN, PS), F32)
    both, first, last = pl.pallas_call(
        beside_kernel,
        out_shape=(jax.ShapeDtypeStruct((2, 2, PS, PS), F32), strip, strip),
        in_specs=[VMEM] * 3,
        out_specs=(VMEM,) * 3,
        compiler_params=pltpu.CompilerParams(vmem_limit_bytes=2 << 20),
        name="beside",
    )(block, right, left)
    return (shifted(last, (-1, 0)), both, shifted(first, (1, 0))), modes


def sum_columns(full, from_left, from_right):
    own = full[:3] + by_side(from_left, from_right)
    beside = full[3:] + by_side(from_right, from_left)
    return jnp.stack([own, beside], axis=1)


def inside_object():
    a, b = lax.axis_index("row"), lax.axis_index("col")
    place = a * TILE - MARGIN + lax.iota(jnp.int32, EXT)
    rows = (place >= 0) & (place < lax.axis_size("row") * TILE)
    lane = lax.iota(jnp.int32, PS)
    beside = ((lane < MARGIN) & (b < lax.axis_size("col") - 1)) | ((lane >= MARGIN) & (b > 0))
    cols = jnp.stack([jnp.ones_like(beside), beside])
    return rows[None, :, None] & cols[:, None, :]


def fold(up, mid, down):
    edges = jnp.concatenate([shifted(up, (-1, 0)), shifted(down, (1, 0))], axis=1)
    mid = mid + edges
    beside = mid[3:]
    return mid[:3] + by_side(shifted(beside, (0, -1)), shifted(beside, (0, 1)))


def shards(object_field, probe_modes, coefficients, offsets, counts, measured):
    tables = jnp.asarray(dft_constants())
    offs = offsets[0, 0].T
    photons = measured[0, 0]
    coef = coefficients[0, 0].T
    rows, cols = lax.axis_size("row"), lax.axis_size("col")
    core = lax.axis_index("row") % 2
    half = core.reshape(1)
    groups = [[a * cols + b for a in range(k, rows, 2) for b in range(cols)] for k in range(2)]
    mates = [(a, a ^ 1) for a in range(rows)]
    place = lax.axis_index("row") // 2 * cols + lax.axis_index("col")

    def exchange(x):
        return lax.all_to_all(x, ("row", "col"), 0, 0, axis_index_groups=groups, tiled=True)

    modes = probe_modes.transpose(2, 0, 1, 3).reshape(PS, MODES, 2 * PS)
    mine = lax.dynamic_index_in_dim(modes, core * ROWS + place, 0, keepdims=False)
    pieces, modes = extend(object_field, modes)
    ext = jnp.concatenate(pieces, axis=2)
    for iteration in range(ITERS):
        final = iteration == ITERS - 1
        if iteration == 0:
            probe_r, probe_i = mix_probes(jnp.zeros_like(half), counts, modes, coef)
        else:
            probe_r, probe_i = mix_probes(half * ROWS, counts, near, coef)
            probe_r, probe_i = mix_probes((1 - half) * ROWS, counts, far, coef, probe_r, probe_i)
        up, mid, down, cross_r, cross_i, powers, kept, given = waves(
            half, counts, offs, pieces, photons, probe_r, probe_i, coef, tables, MARGIN if final else PS
        )
        if final:
            sent = kept + lax.ppermute(given, "row", mates)
            got = exchange(sent)
            coef = new_coefficients(cross_r, cross_i, powers, modes, coef)
            got, coef = lax.optimization_barrier((got, coef))
            mine, copies = update_row(got, mine)
            near = exchange(copies)
        else:
            from_above = shifted(up, (-1, 0))
            from_below = shifted(down, (1, 0))
            sent = kept + lax.ppermute(given, "row", mates)
            got = exchange(sent)
            full, to_right, to_left = sum_rows(up, down, from_above, from_below)
            from_left = shifted(to_right, (0, -1))
            from_right = shifted(to_left, (0, 1))
            mine, copies = update_row(got, mine)
            copies, cross_r = lax.optimization_barrier((copies, cross_r))
            coef = new_coefficients(cross_r, cross_i, powers, modes, coef)
            near = exchange(copies)
        far = lax.ppermute(near, "row", mates)
        modes = jnp.where(
            core == 0, jnp.concatenate([near, far]), jnp.concatenate([far, near])
        )
        if final:
            total = fold(up, mid, down)
            object_field = ext[:, 0, MARGIN:-MARGIN] + total[0:2] / (total[2:3] + 1.0)
        else:
            total = sum_columns(full, from_left, from_right)
            step = total[0:2] / (total[2:3] + 1.0)
            ext = ext + jnp.where(inside_object()[None], step, 0.0)
            pieces = (ext,)
    probe_modes = modes.reshape(PS, MODES, 2, PS).transpose(1, 2, 0, 3)
    return (object_field, probe_modes, coef.T[None, None])


def solution(mesh):
    placed = (
        P(None, "row", "col"),
        P(),
        P("row", "col", None, None),
        P("row", "col", None, None),
        P("row", "col"),
        P("row", "col", None, None, None),
    )
    return jax.shard_map(
        shards,
        mesh=mesh,
        in_specs=placed,
        out_specs=(P(None, "row", "col"), P(), P("row", "col", None, None)),
        check_vma=False,
    )
```

profile of v0, /device:TPU:2, one launch (start us, length us, event | category | flops | bytes accessed | tf_op | source)
XLA Modules:
  0.0 179.9 jit_solution(13645145132092285880)
XLA Ops:
  0.7 6.0 %collective-permute-start = (f32[2,128,128]{2,1,0:T(8,128)}, f32[2,128,128]{2,1,0:T(8,128)S(1)}, u32[]{:S(2)}, u32[]{:S(2)}) collective-permute-start(f32[2,128,128]{2,1,0:T(8,128)} %block.1), channel_id=1, source_target_pairs={{1,0},{2,1},{3,2},{4,3},{5,4},{6,5},{7,6},{8,7},{9,8},{10,9},{11,1... | collective-permute-start | bytes 393224 | tf_op jit(solution)/shard_map/ppermute | solution.py:412
  10.5 5.4 %collective-permute-done.1.left = f32[2,128,128]{2,1,0:T(8,128)S(1)} collective-permute-done((f32[2,128,128]{2,1,0:T(8,128)}, f32[2,128,128]{2,1,0:T(8,128)S(1)}, u32[]{:S(2)}, u32[]{:S(2)}) %collective-permute-start.1) | collective-permute-done | bytes 131104 | tf_op jit(solution)/shard_map/ppermute | solution.py:412
  19.9 2.8 %probes.3 = (f32[4224,128]{1,0:T(8,128)S(1)}, f32[4224,128]{1,0:T(8,128)S(1)}) custom-call(s32[1]{0:T(128)} %constant.62.clone.1.base, s32[1,1]{1,0:T(1,128)S(6)} %copy.22.counts, f32[128,8,256]{2,1,0:T(8,128)S(1)} %bitcast.35, f32[8,32]{1,0:T(8,128)S(1)} %bitcast.41), custom_call_target="tpu_custom_call" | custom-call | tf_op jit(solution)/shard_map/probes/pallas_call | solution.py:306
  24.4 15.4 %waves.2 = (f32[6,128,128]{2,1,0:T(8,128)}, f32[6,8,128]{2,1,0:T(8,128)}, f32[6,128,128]{2,1,0:T(8,128)}, f32[4224,128]{1,0:T(8,128)}, f32[4224,128]{1,0:T(8,128...) custom-call(s32[1]{0:T(128)} %bitcast.2.half, s32[1,1]{1,0:T(1,128)S(6)} %copy.22.counts, ...), custom_call_target="tpu_custom_call" | custom-call | tf_op jit(solution)/shard_map/waves/pallas_call | solution.py:335
  39.8 3.5 %collective-permute-start.8 = (f32[64,8,384]{2,1,0:T(8,128)S(1)}, f32[64,8,384]{2,1,0:T(8,128)S(1)}, u32[]{:S(2)}, u32[]{:S(2)}) collective-permute-start(f32[64,8,384]{2,1,0:T(8,128)S(1)} %get-tuple-element.54), channel_id=1, source_target_pairs={{0,16},{16,0},{32,48},{48,32},{64,80},{80,64},{96,112},{112,96},{1... | collective-permute-start | bytes 2359304 | tf_op jit(solution)/shard_map/ppermute | solution.py:498
  46.3 7.9 %all-to-all-start = ((f32[64,8,384]{2,1,0:T(8,128)}), f32[64,8,384]{2,1,0:T(8,128)}, u32[]{:S(2)}, u32[]{:S(2)}) async-start(f32[64,8,384]{2,1,0:T(8,128)} %add.70), calls=%async_computation | async-start | bytes 1572864 | tf_op jit(solution)/shard_map/all_to_all | solution.py:472
  54.2 2.5 %collective-permute-start.4 = (f32[6,128,128]{2,1,0:T(8,128)}, f32[6,128,128]{2,1,0:T(8,128)}, u32[]{:S(2)}, u32[]{:S(2)}) collective-permute-start(f32[6,128,128]{2,1,0:T(8,128)} %get-tuple-element.48.up), channel_id=1, source_target_pairs={{0,16},{1,17},{2,18},{3,19},{4,20},{5,21},{6,22},{7,23},{8,24},{9,... | collective-permute-start | bytes 1179656 | tf_op jit(solution)/shard_map/ppermute | solution.py:412
  58.0 11.7 %all-to-all-done.got = f32[64,8,384]{2,1,0:T(8,128)} async-done(((f32[64,8,384]{2,1,0:T(8,128)}), f32[64,8,384]{2,1,0:T(8,128)}, u32[]{:S(2)}, u32[]{:S(2)}) %all-to-all-start) | async-done | bytes 786464 | tf_op jit(solution)/shard_map/all_to_all | solution.py:472
  69.7 2.1 %update.2 = (f32[8,256]{1,0:T(8,128)S(1)}, f32[64,8,256]{2,1,0:T(8,128)}) custom-call(f32[64,8,384]{2,1,0:T(8,128)} %all-to-all-done.got, f32[8,256]{1,0:T(8,128)S(1)} %dynamic-slice_bitcast_fusion.mine), custom_call_target="tpu_custom_call" | custom-call | tf_op jit(solution)/shard_map/update/pallas_call | solution.py:391
  71.8 5.7 %all-to-all-start.1 = ((f32[64,8,256]{2,1,0:T(8,128)}), f32[64,8,256]{2,1,0:T(8,128)S(1)}, u32[]{:S(2)}, u32[]{:S(2)}) async-start(f32[64,8,256]{2,1,0:T(8,128)} %get-tuple-element.57), calls=%async_computation.1 | async-start | bytes 1048576 | tf_op jit(solution)/shard_map/all_to_all | solution.py:472
  79.5 2.0 %rows.1 = (f32[6,256,128]{2,1,0:T(8,128)S(1)}, f32[3,256,128]{2,1,0:T(8,128)}, f32[3,256,128]{2,1,0:T(8,128)S(1)}) custom-call(f32[6,128,128]{2,1,0:T(8,128)S(1)} %copy-done.8, f32[6,128,128]{2,1,0:T(8,128)S(1)} %copy-done.9, f32[6,128,128]{2,1,0:T(8,128)} %collective-permute-done.4.from_above, f32[6,128,128]{2,1,0:T(8,128)} %collective-permute-done.5.from_below), custom_call_target="tpu_custom_call" | custom-call | tf_op jit(solution)/shard_map/rows/pallas_call | solution.py:319
  82.4 3.4 %collective-permute-start.6 = (f32[3,256,128]{2,1,0:T(8,128)}, f32[3,256,128]{2,1,0:T(8,128)}, u32[]{:S(2)}, u32[]{:S(2)}) collective-permute-start(f32[3,256,128]{2,1,0:T(8,128)} %get-tuple-element.51), channel_id=1, source_target_pairs={{0,1},{1,2},{2,3},{3,4},{4,5},{5,6},{6,7},{7,8},{8,9},{9,10},{10,1... | collective-permute-start | bytes 1179656 | tf_op jit(solution)/shard_map/ppermute | solution.py:412
  85.8 4.6 %collective-permute-start.7 = (f32[3,256,128]{2,1,0:T(8,128)S(1)}, f32[3,256,128]{2,1,0:T(8,128)}, u32[]{:S(2)}, u32[]{:S(2)}) collective-permute-start(f32[3,256,128]{2,1,0:T(8,128)S(1)} %get-tuple-element.52), channel_id=1, source_target_pairs={{1,0},{2,1},{3,2},{4,3},{5,4},{6,5},{7,6},{8,7},{9,8},{10,9},{11,1... | collective-permute-start | bytes 1179656 | tf_op jit(solution)/shard_map/ppermute | solution.py:412
  90.8 5.5 %collective-permute-done.6 = f32[3,256,128]{2,1,0:T(8,128)} collective-permute-done((f32[3,256,128]{2,1,0:T(8,128)}, f32[3,256,128]{2,1,0:T(8,128)}, u32[]{:S(2)}, u32[]{:S(2)}) %collective-permute-start.6) | collective-permute-done | bytes 393248 | tf_op jit(solution)/shard_map/ppermute | solution.py:412
  99.5 5.8 %coefs.2.coef.refs_4_ = f32[8,32]{1,0:T(8,128)} custom-call(f32[4224,128]{1,0:T(8,128)} %get-tuple-element.58.cross_r, f32[4224,128]{1,0:T(8,128)} %get-tuple-element.59.cross_i, f32[4224,128]{1,0:T(8,128)} %get-tuple-element.60.powers, f32[128,8,256]{2,1,0:T(8,128)} %bitcast.37, f32[8,32]{1,0:T(8,128)} %bitcast.40), custom_call_target="tpu_custom_call" | custom-call | tf_op jit(solution)/shard_map/coefs/pallas_call | solution.py:370
  109.0 15.0 %waves.3 = (f32[6,64,128]{2,1,0:T(8,128)}, f32[6,128,128]{2,1,0:T(8,128)}, f32[6,64,128]{2,1,0:T(8,128)}, f32[4224,128]{1,0:T(8,128)}, f32[4224,128]{1,0:T(8,128...) custom-call(s32[1]{0:T(128)} %bitcast.2.half, s32[1,1]{1,0:T(1,128)S(6)} %copy.22.counts, ...), custom_call_target="tpu_custom_call" | custom-call | tf_op jit(solution)/shard_map/waves/pallas_call | solution.py:335
  124.1 2.3 %collective-permute-done.14 = f32[64,8,384]{2,1,0:T(8,128)S(1)} collective-permute-done((f32[64,8,384]{2,1,0:T(8,128)S(1)}, f32[64,8,384]{2,1,0:T(8,128)S(1)}, u32[]{:S(2)}, u32[]{:S(2)}) %collective-permute-start.14) | collective-permute-done | bytes 786464 | tf_op jit(solution)/shard_map/ppermute | solution.py:489
  127.4 11.7 %all-to-all-start.2 = ((f32[64,8,384]{2,1,0:T(8,128)}), f32[64,8,384]{2,1,0:T(8,128)S(1)}, u32[]{:S(2)}, u32[]{:S(2)}) async-start(f32[64,8,384]{2,1,0:T(8,128)} %add.79), calls=%async_computation.2 | async-start | bytes 1572864 | tf_op jit(solution)/shard_map/all_to_all | solution.py:472
  143.0 5.7 %coefs.3 = f32[8,32]{1,0:T(8,128)} custom-call(f32[4224,128]{1,0:T(8,128)} %get-tuple-element.70.cross_r, f32[4224,128]{1,0:T(8,128)} %get-tuple-element.71.cross_i, f32[4224,128]{1,0:T(8,128)} %get-tuple-element.72.powers, f32[128,8,256]{2,1,0:T(8,128)} %maximum_select_fusion.modes, f32[8,32]{1,0:T(8,128)} %coefs.2.coef.refs_4_), custom_call_target="tpu_custom_call" | custom-call | tf_op jit(solution)/shard_map/coefs/pallas_call | solution.py:370
  148.7 5.8 %all-to-all-done.2.got = f32[64,8,384]{2,1,0:T(8,128)S(1)} async-done(((f32[64,8,384]{2,1,0:T(8,128)}), f32[64,8,384]{2,1,0:T(8,128)S(1)}, u32[]{:S(2)}, u32[]{:S(2)}) %all-to-all-start.2) | async-done | bytes 786464 | tf_op jit(solution)/shard_map/all_to_all | solution.py:472
  155.3 7.4 %all-to-all-start.3 = ((f32[64,8,256]{2,1,0:T(8,128)}), f32[64,8,256]{2,1,0:T(8,128)S(1)}, u32[]{:S(2)}, u32[]{:S(2)}) async-start(f32[64,8,256]{2,1,0:T(8,128)} %get-tuple-element.75), calls=%async_computation.3 | async-start | bytes 1048576 | tf_op jit(solution)/shard_map/all_to_all | solution.py:472
  162.8 3.4 %collective-permute-start.12 = (f32[3,128,128]{2,1,0:T(8,128)S(1)}, f32[3,128,128]{2,1,0:T(8,128)S(1)}, u32[]{:S(2)}, u32[]{:S(2)}) collective-permute-start(f32[3,128,128]{2,1,0:T(8,128)S(1)} %slice.40), channel_id=1, source_target_pairs={{0,1},{1,2},{2,3},{3,4},{4,5},{5,6},{6,7},{7,8},{8,9},{9,10},{10,1... | collective-permute-start | bytes 589832 | tf_op jit(solution)/shard_map/ppermute | solution.py:412
  166.2 4.6 %collective-permute-start.13 = (f32[3,128,128]{2,1,0:T(8,128)S(1)}, f32[3,128,128]{2,1,0:T(8,128)S(1)}, u32[]{:S(2)}, u32[]{:S(2)}) collective-permute-start(f32[3,128,128]{2,1,0:T(8,128)S(1)} %slice.40), channel_id=1, source_target_pairs={{1,0},{2,1},{3,2},{4,3},{5,4},{6,5},{7,6},{8,7},{9,8},{10,9},{11,1... | collective-permute-start | bytes 589832 | tf_op jit(solution)/shard_map/ppermute | solution.py:412
  170.8 4.6 %all-to-all-done.3 = f32[64,8,256]{2,1,0:T(8,128)S(1)} async-done(((f32[64,8,256]{2,1,0:T(8,128)}), f32[64,8,256]{2,1,0:T(8,128)S(1)}, u32[]{:S(2)}, u32[]{:S(2)}) %all-to-all-start.3) | async-done | bytes 524320 | tf_op jit(solution)/shard_map/all_to_all | solution.py:472
  (82 shorter events, 33.4 us)
Async XLA Ops:
  0.7 22.7 %copy-start.13 = (s32[1,1,32,2]{2,3,1,0:T(2,128)S(1)}, s32[1,1,32,2]{2,3,1,0:T(2,128)}, u32[]{:S(2)}) copy-start(s32[1,1,32,2]{2,3,1,0:T(2,128)} %param.10) | copy-start | bytes 772
  0.7 22.7 %copy-start.1 = (s32[1,1,32,128,128]{4,3,2,1,0:T(8,128)S(1)}, s32[1,1,32,128,128]{4,3,2,1,0:T(8,128)}, u32[]{:S(2)}) copy-start(s32[1,1,32,128,128]{4,3,2,1,0:T(8,128)} %param.12) | copy-start | bytes 6291460
  0.7 9.8 %collective-permute-start = (f32[2,128,128]{2,1,0:T(8,128)}, f32[2,128,128]{2,1,0:T(8,128)S(1)}, u32[]{:S(2)}, u32[]{:S(2)}) collective-permute-start(f32[2,128,128]{2,1,0:T(8,128)} %block.1), channel_id=1, source_target_pairs={{1,0},{2,1},{3,2},{4,3},{5,4},{6,5},{7,6},{8,7},{9,8},{10,9},{11,1... | collective-permute-start | bytes 393224 | tf_op jit(solution)/shard_map/ppermute | solution.py:412
  6.7 9.2 %collective-permute-start.1 = (f32[2,128,128]{2,1,0:T(8,128)}, f32[2,128,128]{2,1,0:T(8,128)S(1)}, u32[]{:S(2)}, u32[]{:S(2)}) collective-permute-start(f32[2,128,128]{2,1,0:T(8,128)} %block.1), channel_id=1, source_target_pairs={{0,1},{1,2},{2,3},{3,4},{4,5},{5,6},{6,7},{7,8},{8,9},{9,10},{10,1... | collective-permute-start | bytes 393224 | tf_op jit(solution)/shard_map/ppermute | solution.py:412
  10.5 47.5 %copy-start = (f32[128,8,2,128]{3,1,2,0:T(8,128)}, f32[128,8,2,128]{3,1,2,0:T(8,128)S(1)}, u32[]{:S(2)}) copy-start(f32[128,8,2,128]{3,1,2,0:T(8,128)S(1)} %copy.19) | copy-start | bytes 3145732
  16.6 6.1 %collective-permute-start.2 = (f32[2,2,64,128]{3,2,1,0:T(8,128)}, f32[2,2,64,128]{3,2,1,0:T(8,128)S(1)}, u32[]{:S(2)}, u32[]{:S(2)}) collective-permute-start(f32[2,2,64,128]{3,2,1,0:T(8,128)} %get-tuple-element.42), channel_id=1, source_target_pairs={{0,16},{1,17},{2,18},{3,19},{4,20},{5,21},{6,22},{7,23},{8,24},{9,... | collective-permute-start | bytes 393224 | tf_op jit(solution)/shard_map/ppermute | solution.py:412
  17.9 5.4 %collective-permute-start.3 = (f32[2,2,64,128]{3,2,1,0:T(8,128)}, f32[2,2,64,128]{3,2,1,0:T(8,128)}, u32[]{:S(2)}, u32[]{:S(2)}) collective-permute-start(f32[2,2,64,128]{3,2,1,0:T(8,128)} %get-tuple-element.44), channel_id=1, source_target_pairs={{16,0},{17,1},{18,2},{19,3},{20,4},{21,5},{22,6},{23,7},{24,8},{25... | collective-permute-start | bytes 393224 | tf_op jit(solution)/shard_map/ppermute | solution.py:412
  39.8 5.4 %collective-permute-start.8 = (f32[64,8,384]{2,1,0:T(8,128)S(1)}, f32[64,8,384]{2,1,0:T(8,128)S(1)}, u32[]{:S(2)}, u32[]{:S(2)}) collective-permute-start(f32[64,8,384]{2,1,0:T(8,128)S(1)} %get-tuple-element.54), channel_id=1, source_target_pairs={{0,16},{16,0},{32,48},{48,32},{64,80},{80,64},{96,112},{112,96},{1... | collective-permute-start | bytes 2359304 | tf_op jit(solution)/shard_map/ppermute | solution.py:498
  46.3 23.4 %all-to-all-start = ((f32[64,8,384]{2,1,0:T(8,128)}), f32[64,8,384]{2,1,0:T(8,128)}, u32[]{:S(2)}, u32[]{:S(2)}) async-start(f32[64,8,384]{2,1,0:T(8,128)} %add.70), calls=%async_computation | async-start | bytes 1572864 | tf_op jit(solution)/shard_map/all_to_all | solution.py:472
  54.2 23.3 %collective-permute-start.4 = (f32[6,128,128]{2,1,0:T(8,128)}, f32[6,128,128]{2,1,0:T(8,128)}, u32[]{:S(2)}, u32[]{:S(2)}) collective-permute-start(f32[6,128,128]{2,1,0:T(8,128)} %get-tuple-element.48.up), channel_id=1, source_target_pairs={{0,16},{1,17},{2,18},{3,19},{4,20},{5,21},{6,22},{7,23},{8,24},{9,... | collective-permute-start | bytes 1179656 | tf_op jit(solution)/shard_map/ppermute | solution.py:412
  56.7 20.8 %collective-permute-start.5 = (f32[6,128,128]{2,1,0:T(8,128)}, f32[6,128,128]{2,1,0:T(8,128)}, u32[]{:S(2)}, u32[]{:S(2)}) collective-permute-start(f32[6,128,128]{2,1,0:T(8,128)} %get-tuple-element.49.down), channel_id=1, source_target_pairs={{16,0},{17,1},{18,2},{19,3},{20,4},{21,5},{22,6},{23,7},{24,8},{25... | collective-permute-start | bytes 1179656 | tf_op jit(solution)/shard_map/ppermute | solution.py:412
  71.8 18.8 %all-to-all-start.1 = ((f32[64,8,256]{2,1,0:T(8,128)}), f32[64,8,256]{2,1,0:T(8,128)S(1)}, u32[]{:S(2)}, u32[]{:S(2)}) async-start(f32[64,8,256]{2,1,0:T(8,128)} %get-tuple-element.57), calls=%async_computation.1 | async-start | bytes 1048576 | tf_op jit(solution)/shard_map/all_to_all | solution.py:472
  82.4 13.9 %collective-permute-start.6 = (f32[3,256,128]{2,1,0:T(8,128)}, f32[3,256,128]{2,1,0:T(8,128)}, u32[]{:S(2)}, u32[]{:S(2)}) collective-permute-start(f32[3,256,128]{2,1,0:T(8,128)} %get-tuple-element.51), channel_id=1, source_target_pairs={{0,1},{1,2},{2,3},{3,4},{4,5},{5,6},{6,7},{7,8},{8,9},{9,10},{10,1... | collective-permute-start | bytes 1179656 | tf_op jit(solution)/shard_map/ppermute | solution.py:412
  85.8 11.2 %collective-permute-start.7 = (f32[3,256,128]{2,1,0:T(8,128)S(1)}, f32[3,256,128]{2,1,0:T(8,128)}, u32[]{:S(2)}, u32[]{:S(2)}) collective-permute-start(f32[3,256,128]{2,1,0:T(8,128)S(1)} %get-tuple-element.52), channel_id=1, source_target_pairs={{1,0},{2,1},{3,2},{4,3},{5,4},{6,5},{7,6},{8,7},{9,8},{10,9},{11,1... | collective-permute-start | bytes 1179656 | tf_op jit(solution)/shard_map/ppermute | solution.py:412
  90.6 16.9 %collective-permute-start.9 = (f32[64,8,256]{2,1,0:T(8,128)S(1)}, f32[64,8,256]{2,1,0:T(8,128)S(1)}, u32[]{:S(2)}, u32[]{:S(2)}) collective-permute-start(f32[64,8,256]{2,1,0:T(8,128)S(1)} %all-to-all-done.1.modes), channel_id=1, source_target_pairs={{0,16},{16,0},{32,48},{48,32},{64,80},{80,64},{96,112},{112,96},{1... | collective-permute-start | bytes 1572872 | tf_op jit(solution)/shard_map/ppermute | solution.py:507
  124.0 2.4 %collective-permute-start.14 = (f32[64,8,384]{2,1,0:T(8,128)S(1)}, f32[64,8,384]{2,1,0:T(8,128)S(1)}, u32[]{:S(2)}, u32[]{:S(2)}) collective-permute-start(f32[64,8,384]{2,1,0:T(8,128)S(1)} %get-tuple-element.69), channel_id=1, source_target_pairs={{0,16},{16,0},{32,48},{48,32},{64,80},{80,64},{96,112},{112,96},{1... | collective-permute-start | bytes 2359304 | tf_op jit(solution)/shard_map/ppermute | solution.py:489
  127.4 27.1 %all-to-all-start.2 = ((f32[64,8,384]{2,1,0:T(8,128)}), f32[64,8,384]{2,1,0:T(8,128)S(1)}, u32[]{:S(2)}, u32[]{:S(2)}) async-start(f32[64,8,384]{2,1,0:T(8,128)} %add.79), calls=%async_computation.2 | async-start | bytes 1572864 | tf_op jit(solution)/shard_map/all_to_all | solution.py:472
  139.1 23.6 %collective-permute-start.10 = (f32[6,64,128]{2,1,0:T(8,128)S(1)}, f32[6,64,128]{2,1,0:T(8,128)S(1)}, u32[]{:S(2)}, u32[]{:S(2)}) collective-permute-start(f32[6,64,128]{2,1,0:T(8,128)S(1)} %copy-done.16), channel_id=1, source_target_pairs={{0,16},{1,17},{2,18},{3,19},{4,20},{5,21},{6,22},{7,23},{8,24},{9,... | collective-permute-start | bytes 589832 | tf_op jit(solution)/shard_map/ppermute | solution.py:412
  140.6 22.1 %collective-permute-start.11 = (f32[6,64,128]{2,1,0:T(8,128)S(1)}, f32[6,64,128]{2,1,0:T(8,128)S(1)}, u32[]{:S(2)}, u32[]{:S(2)}) collective-permute-start(f32[6,64,128]{2,1,0:T(8,128)S(1)} %copy-done.15), channel_id=1, source_target_pairs={{16,0},{17,1},{18,2},{19,3},{20,4},{21,5},{22,6},{23,7},{24,8},{25... | collective-permute-start | bytes 589832 | tf_op jit(solution)/shard_map/ppermute | solution.py:412
  143.0 19.7 %copy-start.14 = (f32[6,128,128]{2,1,0:T(8,128)S(1)}, f32[6,128,128]{2,1,0:T(8,128)}, u32[]{:S(2)}) copy-start(f32[6,128,128]{2,1,0:T(8,128)} %get-tuple-element.65) | copy-start | bytes 1179652
  155.3 20.1 %all-to-all-start.3 = ((f32[64,8,256]{2,1,0:T(8,128)}), f32[64,8,256]{2,1,0:T(8,128)S(1)}, u32[]{:S(2)}, u32[]{:S(2)}) async-start(f32[64,8,256]{2,1,0:T(8,128)} %get-tuple-element.75), calls=%async_computation.3 | async-start | bytes 1048576 | tf_op jit(solution)/shard_map/all_to_all | solution.py:472
  162.8 14.0 %collective-permute-start.12 = (f32[3,128,128]{2,1,0:T(8,128)S(1)}, f32[3,128,128]{2,1,0:T(8,128)S(1)}, u32[]{:S(2)}, u32[]{:S(2)}) collective-permute-start(f32[3,128,128]{2,1,0:T(8,128)S(1)} %slice.40), channel_id=1, source_target_pairs={{0,1},{1,2},{2,3},{3,4},{4,5},{5,6},{6,7},{7,8},{8,9},{9,10},{10,1... | collective-permute-start | bytes 589832 | tf_op jit(solution)/shard_map/ppermute | solution.py:412
  166.2 10.6 %collective-permute-start.13 = (f32[3,128,128]{2,1,0:T(8,128)S(1)}, f32[3,128,128]{2,1,0:T(8,128)S(1)}, u32[]{:S(2)}, u32[]{:S(2)}) collective-permute-start(f32[3,128,128]{2,1,0:T(8,128)S(1)} %slice.40), channel_id=1, source_target_pairs={{1,0},{2,1},{3,2},{4,3},{5,4},{6,5},{7,6},{8,7},{9,8},{10,9},{11,1... | collective-permute-start | bytes 589832 | tf_op jit(solution)/shard_map/ppermute | solution.py:412
  175.4 3.2 %collective-permute-start.15 = (f32[64,8,256]{2,1,0:T(8,128)S(1)}, f32[64,8,256]{2,1,0:T(8,128)S(1)}, u32[]{:S(2)}, u32[]{:S(2)}) collective-permute-start(f32[64,8,256]{2,1,0:T(8,128)S(1)} %all-to-all-done.3), channel_id=1, source_target_pairs={{0,16},{16,0},{32,48},{48,32},{64,80},{80,64},{96,112},{112,96},{1... | collective-permute-start | bytes 1572872 | tf_op jit(solution)/shard_map/ppermute | solution.py:507
  (13 other events, 101.4 us)
where the time goes:
time: 182 us; the launch traced here: 180 us
  starting transfers between devices  69.6 us (38%)
  Pallas kernels  53.3 us (29%)
  waiting for transfers between devices  39.8 us (22%)
  other arithmetic  8.48 us (5%)
  local copies, waits for them, and re-layouts  6.86 us (4%)
  between operations  1.86 us (1%)
    ppermute x12, starting transfers between devices, shifted(): return lax.ppermute(x, ('row', 'col'), pairs)  33 us
    all_to_all x4, starting transfers between devices, exchange(): lax.all_to_all(x, ('row', 'col'), 0, 0, axis_index_groups=groups, tiled=T...  32.8 us
    pallas_call x2, Pallas kernels, waves(): pl.pallas_call(wave_kernel, grid=(PMAX // (2 * PAIRS),), out_shape=(edge,...  30.4 us
    all_to_all x4, waiting for transfers between devices, exchange(): lax.all_to_all(x, ('row', 'col'), 0, 0, axis_index_groups=groups, tiled=T...  22.1 us
    ppermute x12, waiting for transfers between devices, shifted(): return lax.ppermute(x, ('row', 'col'), pairs)  13.6 us
    pallas_call x2, Pallas kernels, new_coefficients(): pl.pallas_call(coef_kernel, grid=(PS // CHUNK,), out_shape=jax.ShapeDtype...  11.5 us
    pallas_call x3, Pallas kernels, mix_probes(): pl.pallas_call(probe_kernel, out_shape=(grid, grid), in_specs=[SMEM, SMEM...  5.72 us
    unnamed x34, local copies, waits for them, and re-layouts  4.65 us
  transfers between devices with their start and end apart: 20, of which 10 were waited for; matrix products, arithmetic and copies ran while one was open for 4% of the time, Pallas kernels for 12%

commit v1 on v0

--- a/solution.py
+++ b/solution.py
@@ -69,7 +69,14 @@
         probe_i[pl.ds(start, PMAX), :] = out[:, PS:]
         return 0
 
-    lax.fori_loop(0, modes.shape[0], rows, 0, unroll=8)
+    lax.fori_loop(0, modes.shape[0], rows, 0, unroll=64)
+
+
+def first_probe_kernel(base, counts, modes, coef, tables, probe_r, probe_i, kept, sem):
+    copy = pltpu.make_async_copy(tables, kept, sem)
+    copy.start()
+    probe_kernel(base, counts, modes, coef, probe_r, probe_i)
+    copy.wait()
 
 
 def wave_kernel(half, counts, offs, *refs):
@@ -142,8 +149,8 @@
         count = jnp.concatenate([photons[2 * j], photons[2 * j + 1]], axis=1).astype(F32)
         far_r = there[:PS]
         far_i = there[PS:]
-        size = jnp.maximum(far_r * far_r + far_i * far_i, 0.25)
-        scale = count * lax.rsqrt(jnp.maximum(count * size, 0.0625)) * 0.03125
+        power_there = jnp.maximum(far_r * far_r + far_i * far_i, 0.25)
+        scale = count * lax.rsqrt(jnp.maximum(count * power_there, 0.0625)) * 0.03125
         return jnp.concatenate([far_r * scale, far_i * scale], axis=0)
 
     def finish(j):
@@ -177,12 +184,19 @@
     pairs = range(PAIRS)
     for j in pairs:
         start(j)
-    x = [dot(triple(wave[j], 1), table(0, 0)) for j in pairs]
+    size = 2 * PS
+    x = []
+    for j in range(0, PAIRS, 2):
+        out = dot(triple(wave[j : j + 2].reshape(2 * size, size), 1), table(0, 0))
+        x += [out[:size], out[size:]]
     x = [dot(table(1, 1), triple(regroup(x[j]), 0)) for j in pairs]
     x = [correct(j, x[j]) for j in pairs]
     x = [dot(table(0, 1), triple(x[j], 0)) for j in pairs]
-    for j in pairs:
-        field[j] = dot(triple(regroup(x[j]), 1), table(1, 0)) - wave[j]
+    for j in range(0, PAIRS, 2):
+        both = jnp.concatenate([regroup(x[j]), regroup(x[j + 1])], axis=0)
+        out = dot(triple(both, 1), table(1, 0))
+        field[j] = out[:size] - wave[j]
+        field[j + 1] = out[size:] - wave[j + 1]
     for j in pairs:
         finish(j)
 
@@ -227,7 +241,7 @@
                 target[y, :, 2 * PS:] = out[:MODES] + out[MODES:]
                 return 0
 
-            lax.fori_loop(0, ROWS, rows, 0, unroll=8)
+            lax.fori_loop(0, ROWS, rows, 0, unroll=16)
         for copy in copies:
             copy.wait()
 
@@ -285,16 +299,21 @@
             last[c, i] = plane[MARGIN:]
 
 
-def rows_kernel(up, down, from_above, from_below, full, to_right, to_left):
+def rows_kernel(
+    down_own, down_beside, above_own, above_beside, up_own, up_beside, below_own, below_beside,
+    own, beside, to_right, to_left,
+):
     lane = lax.broadcasted_iota(jnp.int32, (PS, PS), 1)
-    for c in range(3):
-        for rows, own, other in ((slice(0, PS), down, from_above), (slice(PS, EXT), up, from_below)):
-            centre = own[c] + other[c]
-            beside = own[3 + c] + other[3 + c]
-            full[c, rows] = centre
-            full[3 + c, rows] = beside
-            to_right[c, rows] = jnp.where(lane < MARGIN, beside, centre)
-            to_left[c, rows] = jnp.where(lane < MARGIN, centre, beside)
+    for rows, parts in (
+        (slice(0, PS), (down_own, above_own, down_beside, above_beside)),
+        (slice(PS, EXT), (up_own, below_own, up_beside, below_beside)),
+    ):
+        centre = parts[0][0] + parts[1][0]
+        side = parts[2][0] + parts[3][0]
+        own[0, rows] = centre
+        beside[0, rows] = side
+        to_right[0, rows] = jnp.where(lane < MARGIN, side, centre)
+        to_left[0, rows] = jnp.where(lane < MARGIN, centre, side)
 
 
 SMEM = pl.BlockSpec(memory_space=pltpu.SMEM)
@@ -314,16 +333,34 @@
     )(base, counts, modes, coef, *before)
 
 
+def first_probes(base, counts, modes, coef, tables):
+    grid = jax.ShapeDtypeStruct((PS * LEAD, PS), F32)
+    return pl.pallas_call(
+        first_probe_kernel,
+        out_shape=(grid, grid, jax.ShapeDtypeStruct(tables.shape, tables.dtype)),
+        in_specs=[SMEM, SMEM, VMEM, VMEM, pl.BlockSpec(memory_space=pltpu.HBM)],
+        out_specs=(VMEM, VMEM, VMEM),
+        scratch_shapes=[pltpu.SemaphoreType.DMA],
+        compiler_params=pltpu.CompilerParams(vmem_limit_bytes=2 << 20),
+        name="probes",
+    )(base, counts, modes, coef, tables)
+
+
 def sum_rows(up, down, from_above, from_below):
-    side = jax.ShapeDtypeStruct((3, EXT, PS), F32)
+    whole = jax.ShapeDtypeStruct((3, EXT, PS), F32)
+    near = pl.BlockSpec((1, PS, PS), lambda c: (c, 0, 0))
+    side = pl.BlockSpec((1, PS, PS), lambda c: (3 + c, 0, 0))
     return pl.pallas_call(
         rows_kernel,
-        out_shape=(jax.ShapeDtypeStruct((6, EXT, PS), F32), side, side),
-        in_specs=[VMEM] * 4,
-        out_specs=(VMEM,) * 3,
-        compiler_params=pltpu.CompilerParams(vmem_limit_bytes=2 << 20),
+        grid=(3,),
+        out_shape=(whole,) * 4,
+        in_specs=[near, side] * 4,
+        out_specs=(pl.BlockSpec((1, EXT, PS), lambda c: (c, 0, 0)),) * 4,
+        compiler_params=pltpu.CompilerParams(
+            dimension_semantics=("arbitrary",), vmem_limit_bytes=56 << 20
+        ),
         name="rows",
-    )(up, down, from_above, from_below)
+    )(down, down, from_above, from_above, up, up, from_below, from_below)
 
 
 def waves(half, counts, offs, pieces, photons, probe_r, probe_i, coef, tables, width):
@@ -433,9 +470,9 @@
     return (shifted(last, (-1, 0)), both, shifted(first, (1, 0))), modes
 
 
-def sum_columns(full, from_left, from_right):
-    own = full[:3] + by_side(from_left, from_right)
-    beside = full[3:] + by_side(from_right, from_left)
+def sum_columns(own, beside, from_left, from_right):
+    own = own + by_side(from_left, from_right)
+    beside = beside + by_side(from_right, from_left)
     return jnp.stack([own, beside], axis=1)
 
 
@@ -478,7 +515,9 @@
     for iteration in range(ITERS):
         final = iteration == ITERS - 1
         if iteration == 0:
-            probe_r, probe_i = mix_probes(jnp.zeros_like(half), counts, modes, coef)
+            probe_r, probe_i, tables = first_probes(
+                jnp.zeros_like(half), counts, modes, coef, tables
+            )
         else:
             probe_r, probe_i = mix_probes(half * ROWS, counts, near, coef)
             probe_r, probe_i = mix_probes((1 - half) * ROWS, counts, far, coef, probe_r, probe_i)
@@ -497,7 +536,7 @@
             from_below = shifted(down, (1, 0))
             sent = kept + lax.ppermute(given, "row", mates)
             got = exchange(sent)
-            full, to_right, to_left = sum_rows(up, down, from_above, from_below)
+            own, beside, to_right, to_left = sum_rows(up, down, from_above, from_below)
             from_left = shifted(to_right, (0, -1))
             from_right = shifted(to_left, (0, 1))
             mine, copies = update_row(got, mine)
@@ -512,7 +551,7 @@
             total = fold(up, mid, down)
             object_field = ext[:, 0, MARGIN:-MARGIN] + total[0:2] / (total[2:3] + 1.0)
         else:
-            total = sum_columns(full, from_left, from_right)
+            total = sum_columns(own, beside, from_left, from_right)
             step = total[0:2] / (total[2:3] + 1.0)
             ext = ext + jnp.where(inside_object()[None], step, 0.0)
             pieces = (ext,)

time: 182 us -> 177 us (0.973)
  Pallas kernels: 53.3 us -> 49.1 us
  local copies, waits for them, and re-layouts: 6.86 us -> 4.65 us
    pallas_call x3 -> x2, Pallas kernels: 5.72 us -> 1.1 us  [mix_probes(): pl.pallas_call(probe_kernel, out_shape=(grid, grid), in_specs=[SMEM, SMEM...]
    pallas_call x1 -> x2, Pallas kernels: 2.03 us -> 4.42 us  [the longest x1 3.39 us: sum_rows(): pl.pallas_call(rows_kernel, grid=(3,), out_shape=(whole,) * 4, in_specs=[...]
    unnamed x34, local copies, waits for them, and re-layouts: 4.65 us -> 2.44 us
    pallas_call x2, Pallas kernels: 30.4 us -> 28.3 us  [waves(): pl.pallas_call(wave_kernel, grid=(PMAX // (2 * PAIRS),), out_shape=(edge,...]
  transfers between devices with their start and end apart: 20 -> 20, of which waited for: 10 -> 11; matrix products, arithmetic and copies ran while one was open for 4% -> 4% of each run, Pallas kernels for 12% -> 11%
where the time goes in v1:
time: 177 us; the launch traced here: 175 us
  starting transfers between devices  69.6 us (39%)
  Pallas kernels  49.1 us (28%)
  waiting for transfers between devices  40.9 us (23%)
  other arithmetic  8.39 us (5%)
  local copies, waits for them, and re-layouts  4.65 us (3%)
  between operations  1.85 us (1%)
    ppermute x12, starting transfers between devices, shifted(): return lax.ppermute(x, ('row', 'col'), pairs)  33 us
    all_to_all x4, starting transfers between devices, exchange(): lax.all_to_all(x, ('row', 'col'), 0, 0, axis_index_groups=groups, tiled=T...  32.8 us
    pallas_call x2, Pallas kernels, waves(): pl.pallas_call(wave_kernel, grid=(PMAX // (2 * PAIRS),), out_shape=(edge,...  28.3 us
    all_to_all x4, waiting for transfers between devices, exchange(): lax.all_to_all(x, ('row', 'col'), 0, 0, axis_index_groups=groups, tiled=T...  22.2 us
    ppermute x12, waiting for transfers between devices, shifted(): return lax.ppermute(x, ('row', 'col'), pairs)  14.6 us
    pallas_call x2, Pallas kernels, new_coefficients(): pl.pallas_call(coef_kernel, grid=(PS // CHUNK,), out_shape=jax.ShapeDtype...  11.5 us
    ppermute x2, waiting for transfers between devices, shards(): sent = kept + lax.ppermute(given, 'row', mates)  4.18 us
    ppermute x2, starting transfers between devices, shards(): sent = kept + lax.ppermute(given, 'row', mates)  3.7 us
  transfers between devices with their start and end apart: 20, of which 11 were waited for; matrix products, arithmetic and copies ran while one was open for 4% of the time, Pallas kernels for 11%

profile of v1, /device:TPU:2, one launch (start us, length us, event | category | flops | bytes accessed | tf_op | source)
XLA Modules:
  0.0 174.5 jit_solution(12357628643755513792)
XLA Ops:
  0.7 6.0 %collective-permute-start = (f32[2,128,128]{2,1,0:T(8,128)}, f32[2,128,128]{2,1,0:T(8,128)S(1)}, u32[]{:S(2)}, u32[]{:S(2)}) collective-permute-start(f32[2,128,128]{2,1,0:T(8,128)} %block.1), channel_id=1, source_target_pairs={{1,0},{2,1},{3,2},{4,3},{5,4},{6,5},{7,6},{8,7},{9,8},{10,9},{11,1... | collective-permute-start | bytes 393224 | tf_op jit(solution)/shard_map/ppermute | solution.py:449
  6.7 1.9 %collective-permute-start.1 = (f32[2,128,128]{2,1,0:T(8,128)}, f32[2,128,128]{2,1,0:T(8,128)S(1)}, u32[]{:S(2)}, u32[]{:S(2)}) collective-permute-start(f32[2,128,128]{2,1,0:T(8,128)} %block.1), channel_id=1, source_target_pairs={{0,1},{1,2},{2,3},{3,4},{4,5},{5,6},{6,7},{7,8},{8,9},{9,10},{10,1... | collective-permute-start | bytes 393224 | tf_op jit(solution)/shard_map/ppermute | solution.py:449
  10.5 5.4 %collective-permute-done.1.left = f32[2,128,128]{2,1,0:T(8,128)S(1)} collective-permute-done((f32[2,128,128]{2,1,0:T(8,128)}, f32[2,128,128]{2,1,0:T(8,128)S(1)}, u32[]{:S(2)}, u32[]{:S(2)}) %collective-permute-start.1) | collective-permute-done | bytes 131104 | tf_op jit(solution)/shard_map/ppermute | solution.py:449
  23.3 14.3 %waves.2 = (f32[6,128,128]{2,1,0:T(8,128)}, f32[6,8,128]{2,1,0:T(8,128)}, f32[6,128,128]{2,1,0:T(8,128)}, f32[4224,128]{1,0:T(8,128)}, f32[4224,128]{1,0:T(8,128...) custom-call(s32[1]{0:T(128)} %bitcast.2.half, s32[1,1]{1,0:T(1,128)S(6)} %copy.22.counts, ...), custom_call_target="tpu_custom_call" | custom-call | tf_op jit(solution)/shard_map/waves/pallas_call | solution.py:372
  37.7 3.6 %collective-permute-start.8 = (f32[64,8,384]{2,1,0:T(8,128)S(1)}, f32[64,8,384]{2,1,0:T(8,128)S(1)}, u32[]{:S(2)}, u32[]{:S(2)}) collective-permute-start(f32[64,8,384]{2,1,0:T(8,128)S(1)} %get-tuple-element.58), channel_id=1, source_target_pairs={{0,16},{16,0},{32,48},{48,32},{64,80},{80,64},{96,112},{112,96},{1... | collective-permute-start | bytes 2359304 | tf_op jit(solution)/shard_map/ppermute | solution.py:537
  44.2 7.9 %all-to-all-start = ((f32[64,8,384]{2,1,0:T(8,128)}), f32[64,8,384]{2,1,0:T(8,128)}, u32[]{:S(2)}, u32[]{:S(2)}) async-start(f32[64,8,384]{2,1,0:T(8,128)} %add.70), calls=%async_computation | async-start | bytes 1572864 | tf_op jit(solution)/shard_map/all_to_all | solution.py:509
  52.1 2.5 %collective-permute-start.4 = (f32[6,128,128]{2,1,0:T(8,128)}, f32[6,128,128]{2,1,0:T(8,128)}, u32[]{:S(2)}, u32[]{:S(2)}) collective-permute-start(f32[6,128,128]{2,1,0:T(8,128)} %get-tuple-element.52.up_own.up_beside), channel_id=1, source_target_pairs={{0,16},{1,17},{2,18},{3,19},{4,20},{5,21},{6,22},{7,23},{8,24},{9,... | collective-permute-start | bytes 1179656 | tf_op jit(solution)/shard_map/ppermute | solution.py:449
  56.0 11.7 %all-to-all-done.got = f32[64,8,384]{2,1,0:T(8,128)} async-done(((f32[64,8,384]{2,1,0:T(8,128)}), f32[64,8,384]{2,1,0:T(8,128)}, u32[]{:S(2)}, u32[]{:S(2)}) %all-to-all-start) | async-done | bytes 786464 | tf_op jit(solution)/shard_map/all_to_all | solution.py:509
  67.6 2.1 %update.2 = (f32[8,256]{1,0:T(8,128)S(1)}, f32[64,8,256]{2,1,0:T(8,128)}) custom-call(f32[64,8,384]{2,1,0:T(8,128)} %all-to-all-done.got, f32[8,256]{1,0:T(8,128)S(1)} %dynamic-slice_bitcast_fusion.mine), custom_call_target="tpu_custom_call" | custom-call | tf_op jit(solution)/shard_map/update/pallas_call | solution.py:428
  69.7 5.7 %all-to-all-start.1 = ((f32[64,8,256]{2,1,0:T(8,128)}), f32[64,8,256]{2,1,0:T(8,128)S(1)}, u32[]{:S(2)}, u32[]{:S(2)}) async-start(f32[64,8,256]{2,1,0:T(8,128)} %get-tuple-element.61), calls=%async_computation.1 | async-start | bytes 1048576 | tf_op jit(solution)/shard_map/all_to_all | solution.py:509
  75.5 3.4 %rows.1 = (f32[3,256,128]{2,1,0:T(8,128)}, f32[3,256,128]{2,1,0:T(8,128)}, f32[3,256,128]{2,1,0:T(8,128)}, f32[3,256,128]{2,1,0:T(8,128)}) custom-call(f32[6,128,128]{2,1,0:T(8,128)} %get-tuple-element.51.down_own.down_beside, f32[6,128,128]{2,1,0:T(8,128)} %get-tuple-element.51.down_own.down_beside, ...), custom_call_target="tpu_custom_call" | custom-call | tf_op jit(solution)/shard_map/rows/pallas_call | solution.py:353
  78.9 3.4 %collective-permute-start.6 = (f32[3,256,128]{2,1,0:T(8,128)}, f32[3,256,128]{2,1,0:T(8,128)S(1)}, u32[]{:S(2)}, u32[]{:S(2)}) collective-permute-start(f32[3,256,128]{2,1,0:T(8,128)} %get-tuple-element.54), channel_id=1, source_target_pairs={{0,1},{1,2},{2,3},{3,4},{4,5},{5,6},{6,7},{7,8},{8,9},{9,10},{10,1... | collective-permute-start | bytes 1179656 | tf_op jit(solution)/shard_map/ppermute | solution.py:449
  82.2 4.6 %collective-permute-start.7 = (f32[3,256,128]{2,1,0:T(8,128)}, f32[3,256,128]{2,1,0:T(8,128)}, u32[]{:S(2)}, u32[]{:S(2)}) collective-permute-start(f32[3,256,128]{2,1,0:T(8,128)} %get-tuple-element.55), channel_id=1, source_target_pairs={{1,0},{2,1},{3,2},{4,3},{5,4},{6,5},{7,6},{8,7},{9,8},{10,9},{11,1... | collective-permute-start | bytes 1179656 | tf_op jit(solution)/shard_map/ppermute | solution.py:449
  87.3 6.2 %collective-permute-done.6 = f32[3,256,128]{2,1,0:T(8,128)S(1)} collective-permute-done((f32[3,256,128]{2,1,0:T(8,128)}, f32[3,256,128]{2,1,0:T(8,128)S(1)}, u32[]{:S(2)}, u32[]{:S(2)}) %collective-permute-start.6) | collective-permute-done | bytes 393248 | tf_op jit(solution)/shard_map/ppermute | solution.py:449
  96.1 5.8 %coefs.2.coef.refs_4_ = f32[8,32]{1,0:T(8,128)} custom-call(f32[4224,128]{1,0:T(8,128)} %get-tuple-element.62.cross_r, f32[4224,128]{1,0:T(8,128)} %get-tuple-element.63.cross_i, f32[4224,128]{1,0:T(8,128)} %get-tuple-element.64.powers, f32[128,8,256]{2,1,0:T(8,128)} %bitcast.37, f32[8,32]{1,0:T(8,128)} %bitcast.40), custom_call_target="tpu_custom_call" | custom-call | tf_op jit(solution)/shard_map/coefs/pallas_call | solution.py:407
  104.4 14.0 %waves.3 = (f32[6,64,128]{2,1,0:T(8,128)}, f32[6,128,128]{2,1,0:T(8,128)}, f32[6,64,128]{2,1,0:T(8,128)}, f32[4224,128]{1,0:T(8,128)}, f32[4224,128]{1,0:T(8,128...) custom-call(s32[1]{0:T(128)} %bitcast.2.half, s32[1,1]{1,0:T(1,128)S(6)} %copy.22.counts, ...), custom_call_target="tpu_custom_call" | custom-call | tf_op jit(solution)/shard_map/waves/pallas_call | solution.py:372
  118.6 2.3 %collective-permute-done.14 = f32[64,8,384]{2,1,0:T(8,128)S(1)} collective-permute-done((f32[64,8,384]{2,1,0:T(8,128)S(1)}, f32[64,8,384]{2,1,0:T(8,128)S(1)}, u32[]{:S(2)}, u32[]{:S(2)}) %collective-permute-start.14) | collective-permute-done | bytes 786464 | tf_op jit(solution)/shard_map/ppermute | solution.py:528
  121.9 11.8 %all-to-all-start.2 = ((f32[64,8,384]{2,1,0:T(8,128)}), f32[64,8,384]{2,1,0:T(8,128)S(1)}, u32[]{:S(2)}, u32[]{:S(2)}) async-start(f32[64,8,384]{2,1,0:T(8,128)} %add.79), calls=%async_computation.2 | async-start | bytes 1572864 | tf_op jit(solution)/shard_map/all_to_all | solution.py:509
  137.6 5.7 %coefs.3 = f32[8,32]{1,0:T(8,128)} custom-call(f32[4224,128]{1,0:T(8,128)} %get-tuple-element.74.cross_r, f32[4224,128]{1,0:T(8,128)} %get-tuple-element.75.cross_i, f32[4224,128]{1,0:T(8,128)} %get-tuple-element.76.powers, f32[128,8,256]{2,1,0:T(8,128)} %maximum_select_fusion.modes, f32[8,32]{1,0:T(8,128)} %coefs.2.coef.refs_4_), custom_call_target="tpu_custom_call" | custom-call | tf_op jit(solution)/shard_map/coefs/pallas_call | solution.py:407
  143.2 5.7 %all-to-all-done.2.got = f32[64,8,384]{2,1,0:T(8,128)S(1)} async-done(((f32[64,8,384]{2,1,0:T(8,128)}), f32[64,8,384]{2,1,0:T(8,128)S(1)}, u32[]{:S(2)}, u32[]{:S(2)}) %all-to-all-start.2) | async-done | bytes 786464 | tf_op jit(solution)/shard_map/all_to_all | solution.py:509
  149.9 7.4 %all-to-all-start.3 = ((f32[64,8,256]{2,1,0:T(8,128)}), f32[64,8,256]{2,1,0:T(8,128)S(1)}, u32[]{:S(2)}, u32[]{:S(2)}) async-start(f32[64,8,256]{2,1,0:T(8,128)} %get-tuple-element.79), calls=%async_computation.3 | async-start | bytes 1048576 | tf_op jit(solution)/shard_map/all_to_all | solution.py:509
  157.4 3.4 %collective-permute-start.12 = (f32[3,128,128]{2,1,0:T(8,128)S(1)}, f32[3,128,128]{2,1,0:T(8,128)S(1)}, u32[]{:S(2)}, u32[]{:S(2)}) collective-permute-start(f32[3,128,128]{2,1,0:T(8,128)S(1)} %slice.32), channel_id=1, source_target_pairs={{0,1},{1,2},{2,3},{3,4},{4,5},{5,6},{6,7},{7,8},{8,9},{9,10},{10,1... | collective-permute-start | bytes 589832 | tf_op jit(solution)/shard_map/ppermute | solution.py:449
  160.7 4.6 %collective-permute-start.13 = (f32[3,128,128]{2,1,0:T(8,128)S(1)}, f32[3,128,128]{2,1,0:T(8,128)S(1)}, u32[]{:S(2)}, u32[]{:S(2)}) collective-permute-start(f32[3,128,128]{2,1,0:T(8,128)S(1)} %slice.32), channel_id=1, source_target_pairs={{1,0},{2,1},{3,2},{4,3},{5,4},{6,5},{7,6},{8,7},{9,8},{10,9},{11,1... | collective-permute-start | bytes 589832 | tf_op jit(solution)/shard_map/ppermute | solution.py:449
  165.3 4.7 %all-to-all-done.3 = f32[64,8,256]{2,1,0:T(8,128)S(1)} async-done(((f32[64,8,256]{2,1,0:T(8,128)}), f32[64,8,256]{2,1,0:T(8,128)S(1)}, u32[]{:S(2)}, u32[]{:S(2)}) %all-to-all-start.3) | async-done | bytes 524320 | tf_op jit(solution)/shard_map/all_to_all | solution.py:509
  (82 shorter events, 28.6 us)
Async XLA Ops:
  0.7 22.7 %copy-start.12 = (s32[1,1,32,2]{2,3,1,0:T(2,128)S(1)}, s32[1,1,32,2]{2,3,1,0:T(2,128)}, u32[]{:S(2)}) copy-start(s32[1,1,32,2]{2,3,1,0:T(2,128)} %param.10) | copy-start | bytes 772
  0.7 22.7 %copy-start.1 = (s32[1,1,32,128,128]{4,3,2,1,0:T(8,128)S(1)}, s32[1,1,32,128,128]{4,3,2,1,0:T(8,128)}, u32[]{:S(2)}) copy-start(s32[1,1,32,128,128]{4,3,2,1,0:T(8,128)} %param.12) | copy-start | bytes 6291460
  0.7 9.8 %collective-permute-start = (f32[2,128,128]{2,1,0:T(8,128)}, f32[2,128,128]{2,1,0:T(8,128)S(1)}, u32[]{:S(2)}, u32[]{:S(2)}) collective-permute-start(f32[2,128,128]{2,1,0:T(8,128)} %block.1), channel_id=1, source_target_pairs={{1,0},{2,1},{3,2},{4,3},{5,4},{6,5},{7,6},{8,7},{9,8},{10,9},{11,1... | collective-permute-start | bytes 393224 | tf_op jit(solution)/shard_map/ppermute | solution.py:449
  6.7 9.2 %collective-permute-start.1 = (f32[2,128,128]{2,1,0:T(8,128)}, f32[2,128,128]{2,1,0:T(8,128)S(1)}, u32[]{:S(2)}, u32[]{:S(2)}) collective-permute-start(f32[2,128,128]{2,1,0:T(8,128)} %block.1), channel_id=1, source_target_pairs={{0,1},{1,2},{2,3},{3,4},{4,5},{5,6},{6,7},{7,8},{8,9},{9,10},{10,1... | collective-permute-start | bytes 393224 | tf_op jit(solution)/shard_map/ppermute | solution.py:449
  10.5 45.4 %copy-start = (f32[128,8,2,128]{3,1,2,0:T(8,128)}, f32[128,8,2,128]{3,1,2,0:T(8,128)S(1)}, u32[]{:S(2)}) copy-start(f32[128,8,2,128]{3,1,2,0:T(8,128)S(1)} %copy.19) | copy-start | bytes 3145732
  16.6 5.4 %collective-permute-start.2 = (f32[2,2,64,128]{3,2,1,0:T(8,128)}, f32[2,2,64,128]{3,2,1,0:T(8,128)S(1)}, u32[]{:S(2)}, u32[]{:S(2)}) collective-permute-start(f32[2,2,64,128]{3,2,1,0:T(8,128)} %get-tuple-element.44), channel_id=1, source_target_pairs={{0,16},{1,17},{2,18},{3,19},{4,20},{5,21},{6,22},{7,23},{8,24},{9,... | collective-permute-start | bytes 393224 | tf_op jit(solution)/shard_map/ppermute | solution.py:449
  17.9 5.4 %collective-permute-start.3 = (f32[2,2,64,128]{3,2,1,0:T(8,128)}, f32[2,2,64,128]{3,2,1,0:T(8,128)}, u32[]{:S(2)}, u32[]{:S(2)}) collective-permute-start(f32[2,2,64,128]{3,2,1,0:T(8,128)} %get-tuple-element.46), channel_id=1, source_target_pairs={{16,0},{17,1},{18,2},{19,3},{20,4},{21,5},{22,6},{23,7},{24,8},{25... | collective-permute-start | bytes 393224 | tf_op jit(solution)/shard_map/ppermute | solution.py:449
  37.7 5.5 %collective-permute-start.8 = (f32[64,8,384]{2,1,0:T(8,128)S(1)}, f32[64,8,384]{2,1,0:T(8,128)S(1)}, u32[]{:S(2)}, u32[]{:S(2)}) collective-permute-start(f32[64,8,384]{2,1,0:T(8,128)S(1)} %get-tuple-element.58), channel_id=1, source_target_pairs={{0,16},{16,0},{32,48},{48,32},{64,80},{80,64},{96,112},{112,96},{1... | collective-permute-start | bytes 2359304 | tf_op jit(solution)/shard_map/ppermute | solution.py:537
  44.2 23.4 %all-to-all-start = ((f32[64,8,384]{2,1,0:T(8,128)}), f32[64,8,384]{2,1,0:T(8,128)}, u32[]{:S(2)}, u32[]{:S(2)}) async-start(f32[64,8,384]{2,1,0:T(8,128)} %add.70), calls=%async_computation | async-start | bytes 1572864 | tf_op jit(solution)/shard_map/all_to_all | solution.py:509
  52.1 23.3 %collective-permute-start.4 = (f32[6,128,128]{2,1,0:T(8,128)}, f32[6,128,128]{2,1,0:T(8,128)}, u32[]{:S(2)}, u32[]{:S(2)}) collective-permute-start(f32[6,128,128]{2,1,0:T(8,128)} %get-tuple-element.52.up_own.up_beside), channel_id=1, source_target_pairs={{0,16},{1,17},{2,18},{3,19},{4,20},{5,21},{6,22},{7,23},{8,24},{9,... | collective-permute-start | bytes 1179656 | tf_op jit(solution)/shard_map/ppermute | solution.py:449
  54.6 20.8 %collective-permute-start.5 = (f32[6,128,128]{2,1,0:T(8,128)}, f32[6,128,128]{2,1,0:T(8,128)}, u32[]{:S(2)}, u32[]{:S(2)}) collective-permute-start(f32[6,128,128]{2,1,0:T(8,128)} %get-tuple-element.51.down_own.down_beside), channel_id=1, source_target_pairs={{16,0},{17,1},{18,2},{19,3},{20,4},{21,5},{22,6},{23,7},{24,8},{25... | collective-permute-start | bytes 1179656 | tf_op jit(solution)/shard_map/ppermute | solution.py:449
  69.7 17.4 %all-to-all-start.1 = ((f32[64,8,256]{2,1,0:T(8,128)}), f32[64,8,256]{2,1,0:T(8,128)S(1)}, u32[]{:S(2)}, u32[]{:S(2)}) async-start(f32[64,8,256]{2,1,0:T(8,128)} %get-tuple-element.61), calls=%async_computation.1 | async-start | bytes 1048576 | tf_op jit(solution)/shard_map/all_to_all | solution.py:509
  78.9 14.6 %collective-permute-start.6 = (f32[3,256,128]{2,1,0:T(8,128)}, f32[3,256,128]{2,1,0:T(8,128)S(1)}, u32[]{:S(2)}, u32[]{:S(2)}) collective-permute-start(f32[3,256,128]{2,1,0:T(8,128)} %get-tuple-element.54), channel_id=1, source_target_pairs={{0,1},{1,2},{2,3},{3,4},{4,5},{5,6},{6,7},{7,8},{8,9},{9,10},{10,1... | collective-permute-start | bytes 1179656 | tf_op jit(solution)/shard_map/ppermute | solution.py:449
  82.2 11.5 %collective-permute-start.7 = (f32[3,256,128]{2,1,0:T(8,128)}, f32[3,256,128]{2,1,0:T(8,128)}, u32[]{:S(2)}, u32[]{:S(2)}) collective-permute-start(f32[3,256,128]{2,1,0:T(8,128)} %get-tuple-element.55), channel_id=1, source_target_pairs={{1,0},{2,1},{3,2},{4,3},{5,4},{6,5},{7,6},{8,7},{9,8},{10,9},{11,1... | collective-permute-start | bytes 1179656 | tf_op jit(solution)/shard_map/ppermute | solution.py:449
  87.1 16.1 %collective-permute-start.9 = (f32[64,8,256]{2,1,0:T(8,128)S(1)}, f32[64,8,256]{2,1,0:T(8,128)S(1)}, u32[]{:S(2)}, u32[]{:S(2)}) collective-permute-start(f32[64,8,256]{2,1,0:T(8,128)S(1)} %all-to-all-done.1.modes), channel_id=1, source_target_pairs={{0,16},{16,0},{32,48},{48,32},{64,80},{80,64},{96,112},{112,96},{1... | collective-permute-start | bytes 1572872 | tf_op jit(solution)/shard_map/ppermute | solution.py:546
  118.5 2.4 %collective-permute-start.14 = (f32[64,8,384]{2,1,0:T(8,128)S(1)}, f32[64,8,384]{2,1,0:T(8,128)S(1)}, u32[]{:S(2)}, u32[]{:S(2)}) collective-permute-start(f32[64,8,384]{2,1,0:T(8,128)S(1)} %get-tuple-element.73), channel_id=1, source_target_pairs={{0,16},{16,0},{32,48},{48,32},{64,80},{80,64},{96,112},{112,96},{1... | collective-permute-start | bytes 2359304 | tf_op jit(solution)/shard_map/ppermute | solution.py:528
  121.9 27.1 %all-to-all-start.2 = ((f32[64,8,384]{2,1,0:T(8,128)}), f32[64,8,384]{2,1,0:T(8,128)S(1)}, u32[]{:S(2)}, u32[]{:S(2)}) async-start(f32[64,8,384]{2,1,0:T(8,128)} %add.79), calls=%async_computation.2 | async-start | bytes 1572864 | tf_op jit(solution)/shard_map/all_to_all | solution.py:509
  133.7 23.6 %collective-permute-start.10 = (f32[6,64,128]{2,1,0:T(8,128)S(1)}, f32[6,64,128]{2,1,0:T(8,128)S(1)}, u32[]{:S(2)}, u32[]{:S(2)}) collective-permute-start(f32[6,64,128]{2,1,0:T(8,128)S(1)} %copy-done.16), channel_id=1, source_target_pairs={{0,16},{1,17},{2,18},{3,19},{4,20},{5,21},{6,22},{7,23},{8,24},{9,... | collective-permute-start | bytes 589832 | tf_op jit(solution)/shard_map/ppermute | solution.py:449
  135.2 22.1 %collective-permute-start.11 = (f32[6,64,128]{2,1,0:T(8,128)S(1)}, f32[6,64,128]{2,1,0:T(8,128)S(1)}, u32[]{:S(2)}, u32[]{:S(2)}) collective-permute-start(f32[6,64,128]{2,1,0:T(8,128)S(1)} %copy-done.15), channel_id=1, source_target_pairs={{16,0},{17,1},{18,2},{19,3},{20,4},{21,5},{22,6},{23,7},{24,8},{25... | collective-permute-start | bytes 589832 | tf_op jit(solution)/shard_map/ppermute | solution.py:449
  137.6 19.7 %copy-start.14 = (f32[6,128,128]{2,1,0:T(8,128)S(1)}, f32[6,128,128]{2,1,0:T(8,128)}, u32[]{:S(2)}) copy-start(f32[6,128,128]{2,1,0:T(8,128)} %get-tuple-element.69) | copy-start | bytes 1179652
  149.9 20.1 %all-to-all-start.3 = ((f32[64,8,256]{2,1,0:T(8,128)}), f32[64,8,256]{2,1,0:T(8,128)S(1)}, u32[]{:S(2)}, u32[]{:S(2)}) async-start(f32[64,8,256]{2,1,0:T(8,128)} %get-tuple-element.79), calls=%async_computation.3 | async-start | bytes 1048576 | tf_op jit(solution)/shard_map/all_to_all | solution.py:509
  157.4 14.0 %collective-permute-start.12 = (f32[3,128,128]{2,1,0:T(8,128)S(1)}, f32[3,128,128]{2,1,0:T(8,128)S(1)}, u32[]{:S(2)}, u32[]{:S(2)}) collective-permute-start(f32[3,128,128]{2,1,0:T(8,128)S(1)} %slice.32), channel_id=1, source_target_pairs={{0,1},{1,2},{2,3},{3,4},{4,5},{5,6},{6,7},{7,8},{8,9},{9,10},{10,1... | collective-permute-start | bytes 589832 | tf_op jit(solution)/shard_map/ppermute | solution.py:449
  160.7 10.6 %collective-permute-start.13 = (f32[3,128,128]{2,1,0:T(8,128)S(1)}, f32[3,128,128]{2,1,0:T(8,128)S(1)}, u32[]{:S(2)}, u32[]{:S(2)}) collective-permute-start(f32[3,128,128]{2,1,0:T(8,128)S(1)} %slice.32), channel_id=1, source_target_pairs={{1,0},{2,1},{3,2},{4,3},{5,4},{6,5},{7,6},{8,7},{9,8},{10,9},{11,1... | collective-permute-start | bytes 589832 | tf_op jit(solution)/shard_map/ppermute | solution.py:449
  170.0 3.2 %collective-permute-start.15 = (f32[64,8,256]{2,1,0:T(8,128)S(1)}, f32[64,8,256]{2,1,0:T(8,128)S(1)}, u32[]{:S(2)}, u32[]{:S(2)}) collective-permute-start(f32[64,8,256]{2,1,0:T(8,128)S(1)} %all-to-all-done.3), channel_id=1, source_target_pairs={{0,16},{16,0},{32,48},{48,32},{64,80},{80,64},{96,112},{112,96},{1... | collective-permute-start | bytes 1572872 | tf_op jit(solution)/shard_map/ppermute | solution.py:546
  (13 other events, 114.3 us)

commit v2 on v0

--- a/solution.py
+++ b/solution.py
@@ -69,7 +69,14 @@
         probe_i[pl.ds(start, PMAX), :] = out[:, PS:]
         return 0
 
-    lax.fori_loop(0, modes.shape[0], rows, 0, unroll=8)
+    lax.fori_loop(0, modes.shape[0], rows, 0, unroll=64)
+
+
+def first_probe_kernel(base, counts, modes, coef, tables, probe_r, probe_i, kept, sem):
+    copy = pltpu.make_async_copy(tables, kept, sem)
+    copy.start()
+    probe_kernel(base, counts, modes, coef, probe_r, probe_i)
+    copy.wait()
 
 
 def wave_kernel(half, counts, offs, *refs):
@@ -142,8 +149,8 @@
         count = jnp.concatenate([photons[2 * j], photons[2 * j + 1]], axis=1).astype(F32)
         far_r = there[:PS]
         far_i = there[PS:]
-        size = jnp.maximum(far_r * far_r + far_i * far_i, 0.25)
-        scale = count * lax.rsqrt(jnp.maximum(count * size, 0.0625)) * 0.03125
+        power_there = jnp.maximum(far_r * far_r + far_i * far_i, 0.25)
+        scale = count * lax.rsqrt(jnp.maximum(count * power_there, 0.0625)) * 0.03125
         return jnp.concatenate([far_r * scale, far_i * scale], axis=0)
 
     def finish(j):
@@ -177,12 +184,19 @@
     pairs = range(PAIRS)
     for j in pairs:
         start(j)
-    x = [dot(triple(wave[j], 1), table(0, 0)) for j in pairs]
+    size = 2 * PS
+    x = []
+    for j in range(0, PAIRS, 2):
+        out = dot(triple(wave[j : j + 2].reshape(2 * size, size), 1), table(0, 0))
+        x += [out[:size], out[size:]]
     x = [dot(table(1, 1), triple(regroup(x[j]), 0)) for j in pairs]
     x = [correct(j, x[j]) for j in pairs]
     x = [dot(table(0, 1), triple(x[j], 0)) for j in pairs]
-    for j in pairs:
-        field[j] = dot(triple(regroup(x[j]), 1), table(1, 0)) - wave[j]
+    for j in range(0, PAIRS, 2):
+        both = jnp.concatenate([regroup(x[j]), regroup(x[j + 1])], axis=0)
+        out = dot(triple(both, 1), table(1, 0))
+        field[j] = out[:size] - wave[j]
+        field[j + 1] = out[size:] - wave[j + 1]
     for j in pairs:
         finish(j)
 
@@ -227,7 +241,7 @@
                 target[y, :, 2 * PS:] = out[:MODES] + out[MODES:]
                 return 0
 
-            lax.fori_loop(0, ROWS, rows, 0, unroll=8)
+            lax.fori_loop(0, ROWS, rows, 0, unroll=16)
         for copy in copies:
             copy.wait()
 
@@ -312,6 +326,19 @@
         compiler_params=pltpu.CompilerParams(vmem_limit_bytes=2 << 20),
         name="probes",
     )(base, counts, modes, coef, *before)
+
+
+def first_probes(base, counts, modes, coef, tables):
+    grid = jax.ShapeDtypeStruct((PS * LEAD, PS), F32)
+    return pl.pallas_call(
+        first_probe_kernel,
+        out_shape=(grid, grid, jax.ShapeDtypeStruct(tables.shape, tables.dtype)),
+        in_specs=[SMEM, SMEM, VMEM, VMEM, pl.BlockSpec(memory_space=pltpu.HBM)],
+        out_specs=(VMEM, VMEM, VMEM),
+        scratch_shapes=[pltpu.SemaphoreType.DMA],
+        compiler_params=pltpu.CompilerParams(vmem_limit_bytes=2 << 20),
+        name="probes",
+    )(base, counts, modes, coef, tables)
 
 
 def sum_rows(up, down, from_above, from_below):
@@ -478,7 +505,9 @@
     for iteration in range(ITERS):
         final = iteration == ITERS - 1
         if iteration == 0:
-            probe_r, probe_i = mix_probes(jnp.zeros_like(half), counts, modes, coef)
+            probe_r, probe_i, tables = first_probes(
+                jnp.zeros_like(half), counts, modes, coef, tables
+            )
         else:
             probe_r, probe_i = mix_probes(half * ROWS, counts, near, coef)
             probe_r, probe_i = mix_probes((1 - half) * ROWS, counts, far, coef, probe_r, probe_i)

time: 182 us -> 179 us (0.984)
  Pallas kernels: 53.3 us -> 48.5 us
    pallas_call x3 -> x2, Pallas kernels: 5.72 us -> 1.11 us  [mix_probes(): pl.pallas_call(probe_kernel, out_shape=(grid, grid), in_specs=[SMEM, SMEM...]
    unnamed x34 -> x36, local copies, waits for them, and re-layouts: 4.65 us -> 5.3 us
  transfers between devices with their start and end apart: 20 -> 20, of which waited for: 10 -> 10; matrix products, arithmetic and copies ran while one was open for 4% -> 4% of each run, Pallas kernels for 12% -> 10%
where the time goes in v2:
time: 179 us; the launch traced here: 176 us
  starting transfers between devices  69.6 us (39%)
  Pallas kernels  48.5 us (27%)
  waiting for transfers between devices  40.5 us (23%)
  other arithmetic  8.47 us (5%)
  local copies, waits for them, and re-layouts  7.52 us (4%)
  between operations  1.85 us (1%)
    ppermute x12, starting transfers between devices, shifted(): return lax.ppermute(x, ('row', 'col'), pairs)  33 us
    all_to_all x4, starting transfers between devices, exchange(): lax.all_to_all(x, ('row', 'col'), 0, 0, axis_index_groups=groups, tiled=T...  32.8 us
    pallas_call x2, Pallas kernels, waves(): pl.pallas_call(wave_kernel, grid=(PMAX // (2 * PAIRS),), out_shape=(edge,...  29.1 us
    all_to_all x4, waiting for transfers between devices, exchange(): lax.all_to_all(x, ('row', 'col'), 0, 0, axis_index_groups=groups, tiled=T...  22.1 us
    ppermute x12, waiting for transfers between devices, shifted(): return lax.ppermute(x, ('row', 'col'), pairs)  14.3 us
    pallas_call x2, Pallas kernels, new_coefficients(): pl.pallas_call(coef_kernel, grid=(PS // CHUNK,), out_shape=jax.ShapeDtype...  11.5 us
    unnamed x36, local copies, waits for them, and re-layouts  5.3 us
    ppermute x2, waiting for transfers between devices, shards(): sent = kept + lax.ppermute(given, 'row', mates)  4.18 us
  transfers between devices with their start and end apart: 20, of which 10 were waited for; matrix products, arithmetic and copies ran while one was open for 4% of the time, Pallas kernels for 10%

profile of v2, /device:TPU:2, one launch (start us, length us, event | category | flops | bytes accessed | tf_op | source)
XLA Modules:
  0.0 176.5 jit_solution(18235314993325244969)
XLA Ops:
  0.7 6.0 %collective-permute-start = (f32[2,128,128]{2,1,0:T(8,128)}, f32[2,128,128]{2,1,0:T(8,128)S(1)}, u32[]{:S(2)}, u32[]{:S(2)}) collective-permute-start(f32[2,128,128]{2,1,0:T(8,128)} %block.1), channel_id=1, source_target_pairs={{1,0},{2,1},{3,2},{4,3},{5,4},{6,5},{7,6},{8,7},{9,8},{10,9},{11,1... | collective-permute-start | bytes 393224 | tf_op jit(solution)/shard_map/ppermute | solution.py:439
  6.7 1.9 %collective-permute-start.1 = (f32[2,128,128]{2,1,0:T(8,128)}, f32[2,128,128]{2,1,0:T(8,128)S(1)}, u32[]{:S(2)}, u32[]{:S(2)}) collective-permute-start(f32[2,128,128]{2,1,0:T(8,128)} %block.1), channel_id=1, source_target_pairs={{0,1},{1,2},{2,3},{3,4},{4,5},{5,6},{6,7},{7,8},{8,9},{9,10},{10,1... | collective-permute-start | bytes 393224 | tf_op jit(solution)/shard_map/ppermute | solution.py:439
  10.5 5.4 %collective-permute-done.1.left = f32[2,128,128]{2,1,0:T(8,128)S(1)} collective-permute-done((f32[2,128,128]{2,1,0:T(8,128)}, f32[2,128,128]{2,1,0:T(8,128)S(1)}, u32[]{:S(2)}, u32[]{:S(2)}) %collective-permute-start.1) | collective-permute-done | bytes 131104 | tf_op jit(solution)/shard_map/ppermute | solution.py:439
  23.3 14.7 %waves.2 = (f32[6,128,128]{2,1,0:T(8,128)}, f32[6,8,128]{2,1,0:T(8,128)}, f32[6,128,128]{2,1,0:T(8,128)}, f32[4224,128]{1,0:T(8,128)}, f32[4224,128]{1,0:T(8,128...) custom-call(s32[1]{0:T(128)} %bitcast.2.half, s32[1,1]{1,0:T(1,128)S(6)} %copy.22.counts, ...), custom_call_target="tpu_custom_call" | custom-call | tf_op jit(solution)/shard_map/waves/pallas_call | solution.py:362
  38.1 3.5 %collective-permute-start.8 = (f32[64,8,384]{2,1,0:T(8,128)S(1)}, f32[64,8,384]{2,1,0:T(8,128)S(1)}, u32[]{:S(2)}, u32[]{:S(2)}) collective-permute-start(f32[64,8,384]{2,1,0:T(8,128)S(1)} %get-tuple-element.56), channel_id=1, source_target_pairs={{0,16},{16,0},{32,48},{48,32},{64,80},{80,64},{96,112},{112,96},{1... | collective-permute-start | bytes 2359304 | tf_op jit(solution)/shard_map/ppermute | solution.py:527
  44.6 7.9 %all-to-all-start = ((f32[64,8,384]{2,1,0:T(8,128)}), f32[64,8,384]{2,1,0:T(8,128)}, u32[]{:S(2)}, u32[]{:S(2)}) async-start(f32[64,8,384]{2,1,0:T(8,128)} %add.70), calls=%async_computation | async-start | bytes 1572864 | tf_op jit(solution)/shard_map/all_to_all | solution.py:499
  52.5 2.5 %collective-permute-start.4 = (f32[6,128,128]{2,1,0:T(8,128)}, f32[6,128,128]{2,1,0:T(8,128)}, u32[]{:S(2)}, u32[]{:S(2)}) collective-permute-start(f32[6,128,128]{2,1,0:T(8,128)} %get-tuple-element.50.up), channel_id=1, source_target_pairs={{0,16},{1,17},{2,18},{3,19},{4,20},{5,21},{6,22},{7,23},{8,24},{9,... | collective-permute-start | bytes 1179656 | tf_op jit(solution)/shard_map/ppermute | solution.py:439
  56.3 11.7 %all-to-all-done.got = f32[64,8,384]{2,1,0:T(8,128)} async-done(((f32[64,8,384]{2,1,0:T(8,128)}), f32[64,8,384]{2,1,0:T(8,128)}, u32[]{:S(2)}, u32[]{:S(2)}) %all-to-all-start) | async-done | bytes 786464 | tf_op jit(solution)/shard_map/all_to_all | solution.py:499
  68.0 2.1 %update.2 = (f32[8,256]{1,0:T(8,128)S(1)}, f32[64,8,256]{2,1,0:T(8,128)}) custom-call(f32[64,8,384]{2,1,0:T(8,128)} %all-to-all-done.got, f32[8,256]{1,0:T(8,128)S(1)} %dynamic-slice_bitcast_fusion.mine), custom_call_target="tpu_custom_call" | custom-call | tf_op jit(solution)/shard_map/update/pallas_call | solution.py:418
  70.1 5.7 %all-to-all-start.1 = ((f32[64,8,256]{2,1,0:T(8,128)}), f32[64,8,256]{2,1,0:T(8,128)S(1)}, u32[]{:S(2)}, u32[]{:S(2)}) async-start(f32[64,8,256]{2,1,0:T(8,128)} %get-tuple-element.59), calls=%async_computation.1 | async-start | bytes 1048576 | tf_op jit(solution)/shard_map/all_to_all | solution.py:499
  77.8 2.0 %rows.1 = (f32[6,256,128]{2,1,0:T(8,128)S(1)}, f32[3,256,128]{2,1,0:T(8,128)}, f32[3,256,128]{2,1,0:T(8,128)S(1)}) custom-call(f32[6,128,128]{2,1,0:T(8,128)S(1)} %copy-done.9, f32[6,128,128]{2,1,0:T(8,128)S(1)} %copy-done.10, f32[6,128,128]{2,1,0:T(8,128)} %collective-permute-done.4.from_above, f32[6,128,128]{2,1,0:T(8,128)} %collective-permute-done.5.from_below), custom_call_target="tpu_custom_call" | custom-call | tf_op jit(solution)/shard_map/rows/pallas_call | solution.py:346
  80.7 3.4 %collective-permute-start.6 = (f32[3,256,128]{2,1,0:T(8,128)}, f32[3,256,128]{2,1,0:T(8,128)}, u32[]{:S(2)}, u32[]{:S(2)}) collective-permute-start(f32[3,256,128]{2,1,0:T(8,128)} %get-tuple-element.53), channel_id=1, source_target_pairs={{0,1},{1,2},{2,3},{3,4},{4,5},{5,6},{6,7},{7,8},{8,9},{9,10},{10,1... | collective-permute-start | bytes 1179656 | tf_op jit(solution)/shard_map/ppermute | solution.py:439
  84.1 4.6 %collective-permute-start.7 = (f32[3,256,128]{2,1,0:T(8,128)S(1)}, f32[3,256,128]{2,1,0:T(8,128)}, u32[]{:S(2)}, u32[]{:S(2)}) collective-permute-start(f32[3,256,128]{2,1,0:T(8,128)S(1)} %get-tuple-element.54), channel_id=1, source_target_pairs={{1,0},{2,1},{3,2},{4,3},{5,4},{6,5},{7,6},{8,7},{9,8},{10,9},{11,1... | collective-permute-start | bytes 1179656 | tf_op jit(solution)/shard_map/ppermute | solution.py:439
  89.1 5.5 %collective-permute-done.6 = f32[3,256,128]{2,1,0:T(8,128)} collective-permute-done((f32[3,256,128]{2,1,0:T(8,128)}, f32[3,256,128]{2,1,0:T(8,128)}, u32[]{:S(2)}, u32[]{:S(2)}) %collective-permute-start.6) | collective-permute-done | bytes 393248 | tf_op jit(solution)/shard_map/ppermute | solution.py:439
  97.8 5.8 %coefs.2.coef.refs_4_ = f32[8,32]{1,0:T(8,128)} custom-call(f32[4224,128]{1,0:T(8,128)} %get-tuple-element.60.cross_r, f32[4224,128]{1,0:T(8,128)} %get-tuple-element.61.cross_i, f32[4224,128]{1,0:T(8,128)} %get-tuple-element.62.powers, f32[128,8,256]{2,1,0:T(8,128)} %bitcast.37, f32[8,32]{1,0:T(8,128)} %bitcast.40), custom_call_target="tpu_custom_call" | custom-call | tf_op jit(solution)/shard_map/coefs/pallas_call | solution.py:397
  106.1 14.4 %waves.3 = (f32[6,64,128]{2,1,0:T(8,128)}, f32[6,128,128]{2,1,0:T(8,128)}, f32[6,64,128]{2,1,0:T(8,128)}, f32[4224,128]{1,0:T(8,128)}, f32[4224,128]{1,0:T(8,128...) custom-call(s32[1]{0:T(128)} %bitcast.2.half, s32[1,1]{1,0:T(1,128)S(6)} %copy.22.counts, ...), custom_call_target="tpu_custom_call" | custom-call | tf_op jit(solution)/shard_map/waves/pallas_call | solution.py:362
  120.6 2.3 %collective-permute-done.14 = f32[64,8,384]{2,1,0:T(8,128)S(1)} collective-permute-done((f32[64,8,384]{2,1,0:T(8,128)S(1)}, f32[64,8,384]{2,1,0:T(8,128)S(1)}, u32[]{:S(2)}, u32[]{:S(2)}) %collective-permute-start.14) | collective-permute-done | bytes 786464 | tf_op jit(solution)/shard_map/ppermute | solution.py:518
  123.9 11.8 %all-to-all-start.2 = ((f32[64,8,384]{2,1,0:T(8,128)}), f32[64,8,384]{2,1,0:T(8,128)S(1)}, u32[]{:S(2)}, u32[]{:S(2)}) async-start(f32[64,8,384]{2,1,0:T(8,128)} %add.79), calls=%async_computation.2 | async-start | bytes 1572864 | tf_op jit(solution)/shard_map/all_to_all | solution.py:499
  139.6 5.7 %coefs.3 = f32[8,32]{1,0:T(8,128)} custom-call(f32[4224,128]{1,0:T(8,128)} %get-tuple-element.72.cross_r, f32[4224,128]{1,0:T(8,128)} %get-tuple-element.73.cross_i, f32[4224,128]{1,0:T(8,128)} %get-tuple-element.74.powers, f32[128,8,256]{2,1,0:T(8,128)} %maximum_select_fusion.modes, f32[8,32]{1,0:T(8,128)} %coefs.2.coef.refs_4_), custom_call_target="tpu_custom_call" | custom-call | tf_op jit(solution)/shard_map/coefs/pallas_call | solution.py:397
  145.2 5.8 %all-to-all-done.2.got = f32[64,8,384]{2,1,0:T(8,128)S(1)} async-done(((f32[64,8,384]{2,1,0:T(8,128)}), f32[64,8,384]{2,1,0:T(8,128)S(1)}, u32[]{:S(2)}, u32[]{:S(2)}) %all-to-all-start.2) | async-done | bytes 786464 | tf_op jit(solution)/shard_map/all_to_all | solution.py:499
  151.9 7.4 %all-to-all-start.3 = ((f32[64,8,256]{2,1,0:T(8,128)}), f32[64,8,256]{2,1,0:T(8,128)S(1)}, u32[]{:S(2)}, u32[]{:S(2)}) async-start(f32[64,8,256]{2,1,0:T(8,128)} %get-tuple-element.77), calls=%async_computation.3 | async-start | bytes 1048576 | tf_op jit(solution)/shard_map/all_to_all | solution.py:499
  159.4 3.4 %collective-permute-start.12 = (f32[3,128,128]{2,1,0:T(8,128)S(1)}, f32[3,128,128]{2,1,0:T(8,128)S(1)}, u32[]{:S(2)}, u32[]{:S(2)}) collective-permute-start(f32[3,128,128]{2,1,0:T(8,128)S(1)} %slice.40), channel_id=1, source_target_pairs={{0,1},{1,2},{2,3},{3,4},{4,5},{5,6},{6,7},{7,8},{8,9},{9,10},{10,1... | collective-permute-start | bytes 589832 | tf_op jit(solution)/shard_map/ppermute | solution.py:439
  162.7 4.6 %collective-permute-start.13 = (f32[3,128,128]{2,1,0:T(8,128)S(1)}, f32[3,128,128]{2,1,0:T(8,128)S(1)}, u32[]{:S(2)}, u32[]{:S(2)}) collective-permute-start(f32[3,128,128]{2,1,0:T(8,128)S(1)} %slice.40), channel_id=1, source_target_pairs={{1,0},{2,1},{3,2},{4,3},{5,4},{6,5},{7,6},{8,7},{9,8},{10,9},{11,1... | collective-permute-start | bytes 589832 | tf_op jit(solution)/shard_map/ppermute | solution.py:439
  167.3 4.6 %all-to-all-done.3 = f32[64,8,256]{2,1,0:T(8,128)S(1)} async-done(((f32[64,8,256]{2,1,0:T(8,128)}), f32[64,8,256]{2,1,0:T(8,128)S(1)}, u32[]{:S(2)}, u32[]{:S(2)}) %all-to-all-start.3) | async-done | bytes 524320 | tf_op jit(solution)/shard_map/all_to_all | solution.py:499
  (84 shorter events, 32.1 us)
Async XLA Ops:
  0.7 22.7 %copy-start.14 = (s32[1,1,32,2]{2,3,1,0:T(2,128)S(1)}, s32[1,1,32,2]{2,3,1,0:T(2,128)}, u32[]{:S(2)}) copy-start(s32[1,1,32,2]{2,3,1,0:T(2,128)} %param.10) | copy-start | bytes 772
  0.7 22.7 %copy-start.1 = (s32[1,1,32,128,128]{4,3,2,1,0:T(8,128)S(1)}, s32[1,1,32,128,128]{4,3,2,1,0:T(8,128)}, u32[]{:S(2)}) copy-start(s32[1,1,32,128,128]{4,3,2,1,0:T(8,128)} %param.12) | copy-start | bytes 6291460
  0.7 9.8 %collective-permute-start = (f32[2,128,128]{2,1,0:T(8,128)}, f32[2,128,128]{2,1,0:T(8,128)S(1)}, u32[]{:S(2)}, u32[]{:S(2)}) collective-permute-start(f32[2,128,128]{2,1,0:T(8,128)} %block.1), channel_id=1, source_target_pairs={{1,0},{2,1},{3,2},{4,3},{5,4},{6,5},{7,6},{8,7},{9,8},{10,9},{11,1... | collective-permute-start | bytes 393224 | tf_op jit(solution)/shard_map/ppermute | solution.py:439
  6.7 9.2 %collective-permute-start.1 = (f32[2,128,128]{2,1,0:T(8,128)}, f32[2,128,128]{2,1,0:T(8,128)S(1)}, u32[]{:S(2)}, u32[]{:S(2)}) collective-permute-start(f32[2,128,128]{2,1,0:T(8,128)} %block.1), channel_id=1, source_target_pairs={{0,1},{1,2},{2,3},{3,4},{4,5},{5,6},{6,7},{7,8},{8,9},{9,10},{10,1... | collective-permute-start | bytes 393224 | tf_op jit(solution)/shard_map/ppermute | solution.py:439
  10.5 45.8 %copy-start = (f32[128,8,2,128]{3,1,2,0:T(8,128)}, f32[128,8,2,128]{3,1,2,0:T(8,128)S(1)}, u32[]{:S(2)}) copy-start(f32[128,8,2,128]{3,1,2,0:T(8,128)S(1)} %copy.19) | copy-start | bytes 3145732
  16.6 5.4 %collective-permute-start.2 = (f32[2,2,64,128]{3,2,1,0:T(8,128)}, f32[2,2,64,128]{3,2,1,0:T(8,128)S(1)}, u32[]{:S(2)}, u32[]{:S(2)}) collective-permute-start(f32[2,2,64,128]{3,2,1,0:T(8,128)} %get-tuple-element.43), channel_id=1, source_target_pairs={{0,16},{1,17},{2,18},{3,19},{4,20},{5,21},{6,22},{7,23},{8,24},{9,... | collective-permute-start | bytes 393224 | tf_op jit(solution)/shard_map/ppermute | solution.py:439
  17.9 5.4 %collective-permute-start.3 = (f32[2,2,64,128]{3,2,1,0:T(8,128)}, f32[2,2,64,128]{3,2,1,0:T(8,128)}, u32[]{:S(2)}, u32[]{:S(2)}) collective-permute-start(f32[2,2,64,128]{3,2,1,0:T(8,128)} %get-tuple-element.45), channel_id=1, source_target_pairs={{16,0},{17,1},{18,2},{19,3},{20,4},{21,5},{22,6},{23,7},{24,8},{25... | collective-permute-start | bytes 393224 | tf_op jit(solution)/shard_map/ppermute | solution.py:439
  38.1 5.5 %collective-permute-start.8 = (f32[64,8,384]{2,1,0:T(8,128)S(1)}, f32[64,8,384]{2,1,0:T(8,128)S(1)}, u32[]{:S(2)}, u32[]{:S(2)}) collective-permute-start(f32[64,8,384]{2,1,0:T(8,128)S(1)} %get-tuple-element.56), channel_id=1, source_target_pairs={{0,16},{16,0},{32,48},{48,32},{64,80},{80,64},{96,112},{112,96},{1... | collective-permute-start | bytes 2359304 | tf_op jit(solution)/shard_map/ppermute | solution.py:527
  44.6 23.4 %all-to-all-start = ((f32[64,8,384]{2,1,0:T(8,128)}), f32[64,8,384]{2,1,0:T(8,128)}, u32[]{:S(2)}, u32[]{:S(2)}) async-start(f32[64,8,384]{2,1,0:T(8,128)} %add.70), calls=%async_computation | async-start | bytes 1572864 | tf_op jit(solution)/shard_map/all_to_all | solution.py:499
  52.5 23.3 %collective-permute-start.4 = (f32[6,128,128]{2,1,0:T(8,128)}, f32[6,128,128]{2,1,0:T(8,128)}, u32[]{:S(2)}, u32[]{:S(2)}) collective-permute-start(f32[6,128,128]{2,1,0:T(8,128)} %get-tuple-element.50.up), channel_id=1, source_target_pairs={{0,16},{1,17},{2,18},{3,19},{4,20},{5,21},{6,22},{7,23},{8,24},{9,... | collective-permute-start | bytes 1179656 | tf_op jit(solution)/shard_map/ppermute | solution.py:439
  55.0 20.9 %collective-permute-start.5 = (f32[6,128,128]{2,1,0:T(8,128)}, f32[6,128,128]{2,1,0:T(8,128)}, u32[]{:S(2)}, u32[]{:S(2)}) collective-permute-start(f32[6,128,128]{2,1,0:T(8,128)} %get-tuple-element.51.down), channel_id=1, source_target_pairs={{16,0},{17,1},{18,2},{19,3},{20,4},{21,5},{22,6},{23,7},{24,8},{25... | collective-permute-start | bytes 1179656 | tf_op jit(solution)/shard_map/ppermute | solution.py:439
  70.1 18.8 %all-to-all-start.1 = ((f32[64,8,256]{2,1,0:T(8,128)}), f32[64,8,256]{2,1,0:T(8,128)S(1)}, u32[]{:S(2)}, u32[]{:S(2)}) async-start(f32[64,8,256]{2,1,0:T(8,128)} %get-tuple-element.59), calls=%async_computation.1 | async-start | bytes 1048576 | tf_op jit(solution)/shard_map/all_to_all | solution.py:499
  80.7 13.9 %collective-permute-start.6 = (f32[3,256,128]{2,1,0:T(8,128)}, f32[3,256,128]{2,1,0:T(8,128)}, u32[]{:S(2)}, u32[]{:S(2)}) collective-permute-start(f32[3,256,128]{2,1,0:T(8,128)} %get-tuple-element.53), channel_id=1, source_target_pairs={{0,1},{1,2},{2,3},{3,4},{4,5},{5,6},{6,7},{7,8},{8,9},{9,10},{10,1... | collective-permute-start | bytes 1179656 | tf_op jit(solution)/shard_map/ppermute | solution.py:439
  84.1 11.2 %collective-permute-start.7 = (f32[3,256,128]{2,1,0:T(8,128)S(1)}, f32[3,256,128]{2,1,0:T(8,128)}, u32[]{:S(2)}, u32[]{:S(2)}) collective-permute-start(f32[3,256,128]{2,1,0:T(8,128)S(1)} %get-tuple-element.54), channel_id=1, source_target_pairs={{1,0},{2,1},{3,2},{4,3},{5,4},{6,5},{7,6},{8,7},{9,8},{10,9},{11,1... | collective-permute-start | bytes 1179656 | tf_op jit(solution)/shard_map/ppermute | solution.py:439
  88.8 16.0 %collective-permute-start.9 = (f32[64,8,256]{2,1,0:T(8,128)S(1)}, f32[64,8,256]{2,1,0:T(8,128)S(1)}, u32[]{:S(2)}, u32[]{:S(2)}) collective-permute-start(f32[64,8,256]{2,1,0:T(8,128)S(1)} %all-to-all-done.1.modes), channel_id=1, source_target_pairs={{0,16},{16,0},{32,48},{48,32},{64,80},{80,64},{96,112},{112,96},{1... | collective-permute-start | bytes 1572872 | tf_op jit(solution)/shard_map/ppermute | solution.py:536
  120.5 2.4 %collective-permute-start.14 = (f32[64,8,384]{2,1,0:T(8,128)S(1)}, f32[64,8,384]{2,1,0:T(8,128)S(1)}, u32[]{:S(2)}, u32[]{:S(2)}) collective-permute-start(f32[64,8,384]{2,1,0:T(8,128)S(1)} %get-tuple-element.71), channel_id=1, source_target_pairs={{0,16},{16,0},{32,48},{48,32},{64,80},{80,64},{96,112},{112,96},{1... | collective-permute-start | bytes 2359304 | tf_op jit(solution)/shard_map/ppermute | solution.py:518
  123.9 27.1 %all-to-all-start.2 = ((f32[64,8,384]{2,1,0:T(8,128)}), f32[64,8,384]{2,1,0:T(8,128)S(1)}, u32[]{:S(2)}, u32[]{:S(2)}) async-start(f32[64,8,384]{2,1,0:T(8,128)} %add.79), calls=%async_computation.2 | async-start | bytes 1572864 | tf_op jit(solution)/shard_map/all_to_all | solution.py:499
  135.7 23.6 %collective-permute-start.10 = (f32[6,64,128]{2,1,0:T(8,128)S(1)}, f32[6,64,128]{2,1,0:T(8,128)S(1)}, u32[]{:S(2)}, u32[]{:S(2)}) collective-permute-start(f32[6,64,128]{2,1,0:T(8,128)S(1)} %copy-done.17), channel_id=1, source_target_pairs={{0,16},{1,17},{2,18},{3,19},{4,20},{5,21},{6,22},{7,23},{8,24},{9,... | collective-permute-start | bytes 589832 | tf_op jit(solution)/shard_map/ppermute | solution.py:439
  137.2 22.1 %collective-permute-start.11 = (f32[6,64,128]{2,1,0:T(8,128)S(1)}, f32[6,64,128]{2,1,0:T(8,128)S(1)}, u32[]{:S(2)}, u32[]{:S(2)}) collective-permute-start(f32[6,64,128]{2,1,0:T(8,128)S(1)} %copy-done.16), channel_id=1, source_target_pairs={{16,0},{17,1},{18,2},{19,3},{20,4},{21,5},{22,6},{23,7},{24,8},{25... | collective-permute-start | bytes 589832 | tf_op jit(solution)/shard_map/ppermute | solution.py:439
  139.6 19.7 %copy-start.15 = (f32[6,128,128]{2,1,0:T(8,128)S(1)}, f32[6,128,128]{2,1,0:T(8,128)}, u32[]{:S(2)}) copy-start(f32[6,128,128]{2,1,0:T(8,128)} %get-tuple-element.67) | copy-start | bytes 1179652
  151.9 20.1 %all-to-all-start.3 = ((f32[64,8,256]{2,1,0:T(8,128)}), f32[64,8,256]{2,1,0:T(8,128)S(1)}, u32[]{:S(2)}, u32[]{:S(2)}) async-start(f32[64,8,256]{2,1,0:T(8,128)} %get-tuple-element.77), calls=%async_computation.3 | async-start | bytes 1048576 | tf_op jit(solution)/shard_map/all_to_all | solution.py:499
  159.4 14.0 %collective-permute-start.12 = (f32[3,128,128]{2,1,0:T(8,128)S(1)}, f32[3,128,128]{2,1,0:T(8,128)S(1)}, u32[]{:S(2)}, u32[]{:S(2)}) collective-permute-start(f32[3,128,128]{2,1,0:T(8,128)S(1)} %slice.40), channel_id=1, source_target_pairs={{0,1},{1,2},{2,3},{3,4},{4,5},{5,6},{6,7},{7,8},{8,9},{9,10},{10,1... | collective-permute-start | bytes 589832 | tf_op jit(solution)/shard_map/ppermute | solution.py:439
  162.7 10.6 %collective-permute-start.13 = (f32[3,128,128]{2,1,0:T(8,128)S(1)}, f32[3,128,128]{2,1,0:T(8,128)S(1)}, u32[]{:S(2)}, u32[]{:S(2)}) collective-permute-start(f32[3,128,128]{2,1,0:T(8,128)S(1)} %slice.40), channel_id=1, source_target_pairs={{1,0},{2,1},{3,2},{4,3},{5,4},{6,5},{7,6},{8,7},{9,8},{10,9},{11,1... | collective-permute-start | bytes 589832 | tf_op jit(solution)/shard_map/ppermute | solution.py:439
  172.0 3.2 %collective-permute-start.15 = (f32[64,8,256]{2,1,0:T(8,128)S(1)}, f32[64,8,256]{2,1,0:T(8,128)S(1)}, u32[]{:S(2)}, u32[]{:S(2)}) collective-permute-start(f32[64,8,256]{2,1,0:T(8,128)S(1)} %all-to-all-done.3), channel_id=1, source_target_pairs={{0,16},{16,0},{32,48},{48,32},{64,80},{80,64},{96,112},{112,96},{1... | collective-permute-start | bytes 1572872 | tf_op jit(solution)/shard_map/ppermute | solution.py:536
  (14 other events, 114.9 us)
